TPU v7x, 512 devices: a whole 4x8x8 slice. The times are simulated.
512 devices in a mesh: date: 32 (over x, z), col: 16 (over y, core).
Axes of the slice: x: 4, y: 8, z: 8, core: 2. Of those that a mesh axis runs over, the one named last changes fastest.
Arguments:
- slc: float32 [2, 32, 128, 8192], P(None, 'date', None, 'col'), may hold values from -80 to 80
- offsets: int32 [32, 4], replicated, may hold values from 0 to 6, as said below
Outputs:
- interferogram: float32 [2, 32, 4, 32, 512], P(None, 'date', None, None, 'col')
- coherence: float32 [32, 4, 32, 512], P('date', None, None, 'col')
Inputs may be any that keep to these rules, and one draw needn't show every extreme that they name: Row d lists the offsets of the pairs whose reference date is d; 0 marks an empty slot, the nonzero entries of a row are distinct, and d plus each offset is at most 31. Date 0 has 4 pairs, one of offset 6.
All inputs are finite; a program needn't handle non-finite values.
Results may differ from a plain program's by a relative error of at most 0.0003.
Values sent between devices are 32-bit elements; how exact they have to be, the bound alone decides.
No kernel may reach another device: no remote copies, remote signals or barrier semaphores. Data moves between devices by JAX's collectives and lax.ppermute only.
A program may use at most 64 MiB of HBM per device.

v0:
```python
import jax
import jax.numpy as jnp
from jax import lax
from jax.sharding import PartitionSpec as P

MAX_OFFSET = 6


epsilon = 1e-06


def passed_along(value, axis, by):
    size = lax.axis_size(axis)
    pairs = [(i, i + by) for i in range(size) if 0 <= i + by < size]
    return lax.ppermute(value, axis, pairs)


def with_halo(cells, sides, width):
    for axis, dim in sides:
        count = lax.axis_size(axis)
        ends = count - 1
        head = lax.slice_in_dim(cells, 0, width, axis=dim)
        tail = lax.slice_in_dim(cells, cells.shape[dim] - width, cells.shape[dim], axis=dim)
        cells = jnp.concatenate(
            [
                lax.ppermute(tail, axis, [(i, (i + 1) % count) for i in range(ends)]),
                cells,
                lax.ppermute(head, axis, [((i + 1) % count, i) for i in range(ends)]),
            ],
            axis=dim,
        )
    return cells


def look_sums(master_real, master_imag, partner_real, partner_imag, live_mask):
    prod_real = master_real * partner_real + master_imag * partner_imag
    prod_imag = master_imag * partner_real - master_real * partner_imag
    power_master = master_real * master_real + master_imag * master_imag
    power_partner = partner_real * partner_real + partner_imag * partner_imag
    power_master = jnp.broadcast_to(power_master, prod_real.shape)
    stacked = jnp.stack([prod_real, prod_imag, power_master, power_partner])
    full_shape = stacked.shape
    blocks = stacked.reshape(full_shape[:-2] + (full_shape[-2] // 4, 4, full_shape[-1] // 16, 16))
    looked = jnp.sum(blocks, axis=(-3, -1)) / 64.0
    return looked * live_mask


def coherence_of(padded):
    row_count = padded.shape[-2] - 2
    col_count = padded.shape[-1] - 2
    window_sum = padded[..., 0:row_count, 0:col_count]
    for down_step in range(3):
        for side_step in range(3):
            if down_step or side_step:
                window_sum = (
                    window_sum
                    + padded[
                        ..., down_step : down_step + row_count, side_step : side_step + col_count
                    ]
                )
    magnitude = jnp.sqrt(window_sum[0] * window_sum[0] + window_sum[1] * window_sum[1])
    return magnitude / (jnp.sqrt(window_sum[2] * window_sum[3]) + epsilon)


def shards(slc, offsets):
    date_index = lax.axis_index("date")
    shifted = []
    for offset_step in range(1, MAX_OFFSET + 1):
        shifted.append(passed_along(slc, "date", -offset_step))
    stacked = jnp.concatenate(shifted, axis=1)
    own_offsets = lax.dynamic_slice_in_dim(offsets, date_index, 1, 0)[0]
    live_mask = (own_offsets > 0).astype(jnp.float32)
    picked = jnp.clip(own_offsets - 1, 0, MAX_OFFSET - 1)
    partner = jnp.take(stacked, picked, axis=1)
    local_sums = look_sums(slc[0, 0], slc[1, 0], partner[0], partner[1], live_mask[:, None, None])
    looked = local_sums[:, None]
    padded = with_halo(looked, (("col", 4),), 1)
    padded = jnp.pad(padded, ((0, 0), (0, 0), (0, 0), (1, 1), (0, 0)))
    return (looked[0:2], coherence_of(padded))


def solution(mesh):
    placed = (P(None, "date", None, "col"), P())
    return jax.shard_map(
        shards,
        mesh=mesh,
        in_specs=placed,
        out_specs=(P(None, "date", None, None, "col"), P("date", None, None, "col")),
        check_vma=False,
    )
```

profile of v0, /device:TPU:31, one launch (start us, length us, event | category | flops | bytes accessed | tf_op | source)
XLA Modules:
  0.0 186.2 jit_solution(15372060299853772992)
XLA Ops:
  0.6 0.0 copy-start.2
  0.6 0.0 copy-start.3
  0.7 11.0 %collective-permute-start.3 = (f32[2,1,128,512]{3,2,1,0:T(8,128)}, f32[2,1,128,512]{3,2,1,0:T(8,128)}, u32[]{:S(2)}, u32[]{:S(2)}) collective-permute-start(f32[2,1,128,512]{3,2,1,0:T(8,128)} %param.2), channel_id=1, source_target_pairs={{64,0},{80,16},{96,32},{112,48},{128,64},{144,80},{160,96},{176,11... | collective-permute-start | bytes 1572872 | tf_op jit(solution)/shard_map/ppermute | solution.py:15
  11.7 1.9 %collective-permute-start.2 = (f32[2,1,128,512]{3,2,1,0:T(8,128)}, f32[2,1,128,512]{3,2,1,0:T(8,128)}, u32[]{:S(2)}, u32[]{:S(2)}) collective-permute-start(f32[2,1,128,512]{3,2,1,0:T(8,128)} %param.2), channel_id=1, source_target_pairs={{48,0},{64,16},{80,32},{96,48},{112,64},{128,80},{144,96},{160,112... | collective-permute-start | bytes 1572872 | tf_op jit(solution)/shard_map/ppermute | solution.py:15
  13.6 7.3 %collective-permute-start.1 = (f32[2,1,128,512]{3,2,1,0:T(8,128)}, f32[2,1,128,512]{3,2,1,0:T(8,128)}, u32[]{:S(2)}, u32[]{:S(2)}) collective-permute-start(f32[2,1,128,512]{3,2,1,0:T(8,128)} %param.2), channel_id=1, source_target_pairs={{32,0},{48,16},{64,32},{80,48},{96,64},{112,80},{128,96},{144,112}... | collective-permute-start | bytes 1572872 | tf_op jit(solution)/shard_map/ppermute | solution.py:15
  20.9 2.2 %collective-permute-start = (f32[2,1,128,512]{3,2,1,0:T(8,128)}, f32[2,1,128,512]{3,2,1,0:T(8,128)}, u32[]{:S(2)}, u32[]{:S(2)}) collective-permute-start(f32[2,1,128,512]{3,2,1,0:T(8,128)} %param.2), channel_id=1, source_target_pairs={{16,0},{32,16},{48,32},{64,48},{80,64},{96,80},{112,96},{128,112},... | collective-permute-start | bytes 1572872 | tf_op jit(solution)/shard_map/ppermute | solution.py:15
  23.1 1.9 %collective-permute-start.4 = (f32[2,1,128,512]{3,2,1,0:T(8,128)}, f32[2,1,128,512]{3,2,1,0:T(8,128)}, u32[]{:S(2)}, u32[]{:S(2)}) collective-permute-start(f32[2,1,128,512]{3,2,1,0:T(8,128)} %param.2), channel_id=1, source_target_pairs={{80,0},{96,16},{112,32},{128,48},{144,64},{160,80},{176,96},{192,1... | collective-permute-start | bytes 1572872 | tf_op jit(solution)/shard_map/ppermute | solution.py:15
  25.0 1.8 slice_bitcast_fusion.1
  26.8 0.9 clamp_reduce_fusion
  27.7 0.7 add.103
  28.5 0.0 copy-done.3
  28.5 0.2 select_reduce_fusion
  28.7 74.6 %collective-permute-done = f32[2,1,128,512]{3,2,1,0:T(8,128)} collective-permute-done((f32[2,1,128,512]{3,2,1,0:T(8,128)}, f32[2,1,128,512]{3,2,1,0:T(8,128)}, u32[]{:S(2)}, u32[]{:S(2)}) %collective-permute-start) | collective-permute-done | bytes 524320 | tf_op jit(solution)/shard_map/ppermute | solution.py:15
  103.2 0.0 copy-done.2
  103.2 2.2 %collective-permute-start.5 = (f32[2,1,128,512]{3,2,1,0:T(8,128)S(1)}, f32[2,1,128,512]{3,2,1,0:T(8,128)S(1)}, u32[]{:S(2)}, u32[]{:S(2)}) collective-permute-start(f32[2,1,128,512]{3,2,1,0:T(8,128)S(1)} %copy-done.2), channel_id=1, source_target_pairs={{96,0},{112,16},{128,32},{144,48},{160,64},{176,80},{192,96},{208,... | collective-permute-start | bytes 1572872 | tf_op jit(solution)/shard_map/ppermute | solution.py:15
  105.5 1.9 %constant_dynamic-update-slice_fusion.5 = f32[2,6,128,512]{3,2,1,0:T(8,128)} fusion(f32[2,1,128,512]{3,2,1,0:T(8,128)} %collective-permute-done), kind=kLoop, calls=%fused_computation.41 | loop fusion | bytes 1048576
  107.3 0.0 collective-permute-done.1
  107.3 1.9 %constant_dynamic-update-slice_fusion.4 = f32[2,6,128,512]{3,2,1,0:T(8,128)} fusion(f32[2,6,128,512]{3,2,1,0:T(8,128)} %constant_dynamic-update-slice_fusion.5, f32[2,1,128,512]{3,2,1,0:T(8,128)} %collective-permute-done.1), kind=kLoop, calls=%fused_computation.40 | loop fusion | bytes 1048576
  109.2 0.0 collective-permute-done.2
  109.2 1.9 %constant_dynamic-update-slice_fusion.3 = f32[2,6,128,512]{3,2,1,0:T(8,128)} fusion(f32[2,6,128,512]{3,2,1,0:T(8,128)} %constant_dynamic-update-slice_fusion.4, f32[2,1,128,512]{3,2,1,0:T(8,128)} %collective-permute-done.2), kind=kLoop, calls=%fused_computation.39 | loop fusion | bytes 1048576
  111.1 0.0 collective-permute-done.3
  111.1 1.9 %constant_dynamic-update-slice_fusion.2 = f32[2,6,128,512]{3,2,1,0:T(8,128)} fusion(f32[2,6,128,512]{3,2,1,0:T(8,128)} %constant_dynamic-update-slice_fusion.3, f32[2,1,128,512]{3,2,1,0:T(8,128)} %collective-permute-done.3), kind=kLoop, calls=%fused_computation.38 | loop fusion | bytes 1048576
  113.0 0.0 collective-permute-done.4
  113.0 1.9 %constant_dynamic-update-slice_fusion.1 = f32[2,6,128,512]{3,2,1,0:T(8,128)} fusion(f32[2,6,128,512]{3,2,1,0:T(8,128)} %constant_dynamic-update-slice_fusion.2, f32[2,1,128,512]{3,2,1,0:T(8,128)} %collective-permute-done.4), kind=kLoop, calls=%fused_computation.37 | loop fusion | bytes 1048576
  114.9 4.5 %collective-permute-done.5 = f32[2,1,128,512]{3,2,1,0:T(8,128)S(1)} collective-permute-done((f32[2,1,128,512]{3,2,1,0:T(8,128)S(1)}, f32[2,1,128,512]{3,2,1,0:T(8,128)S(1)}, u32[]{:S(2)}, u32[]{:S(2)}) %collective-permute-start.5) | collective-permute-done | bytes 524320 | tf_op jit(solution)/shard_map/ppermute | solution.py:15
  119.4 0.9 constant_dynamic-update-slice_fusion
  120.2 3.9 %gather_fusion = f32[4,2,128,512]{3,2,1,0:T(8,128)} fusion(f32[2,6,128,512]{3,2,1,0:T(8,128)} %constant_dynamic-update-slice_fusion, s32[1024]{0:T(1024)S(1)} %pad_clamp_fusion), kind=kCustom, calls=%fused_computation | custom fusion | bytes 4194320 | tf_op jit(solution)/shard_map/jit(_take)/gather | solution.py:74
  124.1 0.0 copy-start.1
  124.1 1.9 %select_bitcast_fusion = f32[2,4,128,512]{3,2,0,1:T(8,128)S(1)} fusion(f32[4,2,128,512]{3,2,1,0:T(8,128)} %gather_fusion, pred[4]{0:T(512)(128)(4,1)S(1)} %compare_and_fusion), kind=kLoop, calls=%fused_computation.2 | loop fusion | flops 524288 | bytes 4194308 | tf_op jit(solution)/shard_map/jit(_take)/select_n | solution.py:74
  126.1 0.0 copy-done.1
  126.1 1.8 multiply_add_fusion.1
  127.9 6.2 %stack.12 = f32[1,4,32,4,32,16]{5,4,3,2,1,0:T(8,128)} reshape(f32[1,4,128,512]{3,2,0,1:T(8,128)} %get-tuple-element.2) | data formatting | bytes 2097152 | tf_op jit(solution)/shard_map/stack | solution.py:41
  134.1 6.2 %stack.13 = f32[1,4,32,4,32,16]{5,4,3,2,1,0:T(8,128)} reshape(f32[1,4,128,512]{3,2,0,1:T(8,128)} %get-tuple-element.3) | data formatting | bytes 2097152 | tf_op jit(solution)/shard_map/stack | solution.py:41
  140.3 4.8 %stack.14 = f32[1,4,32,4,32,16]{5,4,3,2,1,0:T(8,128)} reshape(f32[1,4,128,512]{3,2,0,1:T(8,128)S(1)} %get-tuple-element.4) | data formatting | bytes 2097152 | tf_op jit(solution)/shard_map/stack | solution.py:41
  145.1 0.0 copy-start
  145.1 1.1 stack_broadcast_in_dim.3
  146.2 2.3 %copy-done = f32[1,4,32,4,32,16]{5,4,3,2,1,0:T(8,128)S(1)} copy-done((f32[1,4,32,4,32,16]{5,4,3,2,1,0:T(8,128)S(1)}, f32[1,4,32,4,32,16]{5,4,3,2,1,0:T(8,128)}, u32[]{:S(2)}) %copy-start) | copy-done | bytes 1048600
  148.5 9.3 %maximum_reduce_fusion = f32[4,4,32,32]{3,2,1,0:T(8,128)S(1)} fusion(f32[1,4,32,4,32,16]{5,4,3,2,1,0:T(8,128)} %stack.14, f32[1,4,32,4,32,16]{5,4,3,2,1,0:T(8,128)S(1)} %stack_broadcast_in_dim.3, f32[1,4,32,4,32,16]{5,4,3,2,1,0:T(8,128)S(1)} %copy-done, f32[1,4,32,4,32,16]{5,4,3,2,1,0:T(8,128)} %stack.12), kind=kLoop, calls=%fused_computation.1 | loop fusion | flops 4177920 | bytes 4259840 | tf_op jit(solution)/shard_map/reduce_sum | solution.py:44
  157.7 0.1 bitcast_multiply_fusion
  157.8 0.1 fusion.12
  158.0 17.8 %collective-permute-start.6 = (f32[4,1,4,32,1]{4,3,2,1,0:T(8,128)S(1)}, f32[4,1,4,32,1]{4,3,2,1,0:T(8,128)S(1)}, u32[]{:S(2)}, u32[]{:S(2)}) collective-permute-start(f32[4,1,4,32,1]{4,3,2,1,0:T(8,128)S(1)} %get-tuple-element.8), channel_id=1, source_target_pairs={{0,1},{1,2},{2,3},{3,4},{4,5},{5,6},{6,7},{7,8},{8,9},{9,10},{10,1... | collective-permute-start | bytes 6152 | tf_op jit(solution)/shard_map/ppermute | solution.py:26
  175.8 1.9 %collective-permute-start.7 = (f32[4,1,4,32,1]{4,3,2,1,0:T(8,128)S(1)}, f32[4,1,4,32,1]{4,3,2,1,0:T(8,128)S(1)}, u32[]{:S(2)}, u32[]{:S(2)}) collective-permute-start(f32[4,1,4,32,1]{4,3,2,1,0:T(8,128)S(1)} %get-tuple-element.9), channel_id=1, source_target_pairs={{1,0},{2,1},{3,2},{4,3},{5,4},{6,5},{7,6},{8,7},{9,8},{10,9},{11,1... | collective-permute-start | bytes 6152 | tf_op jit(solution)/shard_map/ppermute | solution.py:28
  177.7 0.7 fusion.4
  178.4 0.6 collective-permute-done.6
  179.1 5.6 %collective-permute-done.7 = f32[4,1,4,32,1]{4,3,2,1,0:T(8,128)S(1)} collective-permute-done((f32[4,1,4,32,1]{4,3,2,1,0:T(8,128)S(1)}, f32[4,1,4,32,1]{4,3,2,1,0:T(8,128)S(1)}, u32[]{:S(2)}, u32[]{:S(2)}) %collective-permute-start.7) | collective-permute-done | bytes 2080 | tf_op jit(solution)/shard_map/ppermute | solution.py:28
  184.7 0.2 select_maximum_fusion
  184.9 0.5 slice_add_fusion
  185.5 0.7 fusion.8
  (3 shorter events, 0.0 us)
Async XLA Ops:
  0.6 102.6 %copy-start.2 = (f32[2,1,128,512]{3,2,1,0:T(8,128)S(1)}, f32[2,1,128,512]{3,2,1,0:T(8,128)}, u32[]{:S(2)}) copy-start(f32[2,1,128,512]{3,2,1,0:T(8,128)} %param.2) | copy-start | bytes 1572868
  0.6 27.8 %copy-start.3 = (s32[32,4]{0,1:T(4,128)S(1)}, s32[32,4]{0,1:T(4,128)}, u32[]{:S(2)}) copy-start(s32[32,4]{0,1:T(4,128)} %param.3) | copy-start | bytes 1540
  0.7 110.4 %collective-permute-start.3 = (f32[2,1,128,512]{3,2,1,0:T(8,128)}, f32[2,1,128,512]{3,2,1,0:T(8,128)}, u32[]{:S(2)}, u32[]{:S(2)}) collective-permute-start(f32[2,1,128,512]{3,2,1,0:T(8,128)} %param.2), channel_id=1, source_target_pairs={{64,0},{80,16},{96,32},{112,48},{128,64},{144,80},{160,96},{176,11... | collective-permute-start | bytes 1572872 | tf_op jit(solution)/shard_map/ppermute | solution.py:15
  11.7 97.5 %collective-permute-start.2 = (f32[2,1,128,512]{3,2,1,0:T(8,128)}, f32[2,1,128,512]{3,2,1,0:T(8,128)}, u32[]{:S(2)}, u32[]{:S(2)}) collective-permute-start(f32[2,1,128,512]{3,2,1,0:T(8,128)} %param.2), channel_id=1, source_target_pairs={{48,0},{64,16},{80,32},{96,48},{112,64},{128,80},{144,96},{160,112... | collective-permute-start | bytes 1572872 | tf_op jit(solution)/shard_map/ppermute | solution.py:15
  13.6 93.7 %collective-permute-start.1 = (f32[2,1,128,512]{3,2,1,0:T(8,128)}, f32[2,1,128,512]{3,2,1,0:T(8,128)}, u32[]{:S(2)}, u32[]{:S(2)}) collective-permute-start(f32[2,1,128,512]{3,2,1,0:T(8,128)} %param.2), channel_id=1, source_target_pairs={{32,0},{48,16},{64,32},{80,48},{96,64},{112,80},{128,96},{144,112}... | collective-permute-start | bytes 1572872 | tf_op jit(solution)/shard_map/ppermute | solution.py:15
  20.9 82.3 %collective-permute-start = (f32[2,1,128,512]{3,2,1,0:T(8,128)}, f32[2,1,128,512]{3,2,1,0:T(8,128)}, u32[]{:S(2)}, u32[]{:S(2)}) collective-permute-start(f32[2,1,128,512]{3,2,1,0:T(8,128)} %param.2), channel_id=1, source_target_pairs={{16,0},{32,16},{48,32},{64,48},{80,64},{96,80},{112,96},{128,112},... | collective-permute-start | bytes 1572872 | tf_op jit(solution)/shard_map/ppermute | solution.py:15
  23.1 89.9 %collective-permute-start.4 = (f32[2,1,128,512]{3,2,1,0:T(8,128)}, f32[2,1,128,512]{3,2,1,0:T(8,128)}, u32[]{:S(2)}, u32[]{:S(2)}) collective-permute-start(f32[2,1,128,512]{3,2,1,0:T(8,128)} %param.2), channel_id=1, source_target_pairs={{80,0},{96,16},{112,32},{128,48},{144,64},{160,80},{176,96},{192,1... | collective-permute-start | bytes 1572872 | tf_op jit(solution)/shard_map/ppermute | solution.py:15
  103.2 16.1 %collective-permute-start.5 = (f32[2,1,128,512]{3,2,1,0:T(8,128)S(1)}, f32[2,1,128,512]{3,2,1,0:T(8,128)S(1)}, u32[]{:S(2)}, u32[]{:S(2)}) collective-permute-start(f32[2,1,128,512]{3,2,1,0:T(8,128)S(1)} %copy-done.2), channel_id=1, source_target_pairs={{96,0},{112,16},{128,32},{144,48},{160,64},{176,80},{192,96},{208,... | collective-permute-start | bytes 1572872 | tf_op jit(solution)/shard_map/ppermute | solution.py:15
  124.1 2.0 %copy-start.1 = (f32[128,512]{1,0:T(8,128)S(1)}, f32[128,512]{1,0:T(8,128)}, u32[]{:S(2)}) copy-start(f32[128,512]{1,0:T(8,128)} %get-tuple-element.7) | copy-start | bytes 786436
  145.1 3.4 %copy-start = (f32[1,4,32,4,32,16]{5,4,3,2,1,0:T(8,128)S(1)}, f32[1,4,32,4,32,16]{5,4,3,2,1,0:T(8,128)}, u32[]{:S(2)}) copy-start(f32[1,4,32,4,32,16]{5,4,3,2,1,0:T(8,128)} %stack.13) | copy-start | bytes 3145732
  158.0 21.1 %collective-permute-start.6 = (f32[4,1,4,32,1]{4,3,2,1,0:T(8,128)S(1)}, f32[4,1,4,32,1]{4,3,2,1,0:T(8,128)S(1)}, u32[]{:S(2)}, u32[]{:S(2)}) collective-permute-start(f32[4,1,4,32,1]{4,3,2,1,0:T(8,128)S(1)} %get-tuple-element.8), channel_id=1, source_target_pairs={{0,1},{1,2},{2,3},{3,4},{4,5},{5,6},{6,7},{7,8},{8,9},{9,10},{10,1... | collective-permute-start | bytes 6152 | tf_op jit(solution)/shard_map/ppermute | solution.py:26
  175.8 8.9 %collective-permute-start.7 = (f32[4,1,4,32,1]{4,3,2,1,0:T(8,128)S(1)}, f32[4,1,4,32,1]{4,3,2,1,0:T(8,128)S(1)}, u32[]{:S(2)}, u32[]{:S(2)}) collective-permute-start(f32[4,1,4,32,1]{4,3,2,1,0:T(8,128)S(1)} %get-tuple-element.9), channel_id=1, source_target_pairs={{1,0},{2,1},{3,2},{4,3},{5,4},{6,5},{7,6},{8,7},{9,8},{10,9},{11,1... | collective-permute-start | bytes 6152 | tf_op jit(solution)/shard_map/ppermute | solution.py:28
where the time goes:
time: 187 us; the launch traced here: 186 us
  waiting for transfers between devices  85.4 us (46%)
  starting transfers between devices  46.2 us (25%)
  local copies, waits for them, and re-layouts  35.5 us (19%)
  other arithmetic  18.2 us (10%)
    ppermute x6, waiting for transfers between devices, passed_along(): return lax.ppermute(value, axis, pairs)  79.1 us
    ppermute x6, starting transfers between devices, passed_along(): return lax.ppermute(value, axis, pairs)  26.5 us
    another operation x4, local copies, waits for them, and re-layouts, look_sums(): stacked = jnp.stack([prod_real, prod_imag, power_master, power_partner])  18.2 us
    ppermute x1, starting transfers between devices, with_halo(): lax.ppermute(tail, axis, [(i, (i + 1) % count) for i in range(ends)])  17.8 us
    unnamed x13, local copies, waits for them, and re-layouts  11.7 us
    reduce_sum x1, other arithmetic, look_sums(): looked = jnp.sum(blocks, axis=(-3, -1)) / 64.0  9.26 us
    ppermute x1, waiting for transfers between devices, with_halo(): lax.ppermute(head, axis, [((i + 1) % count, i) for i in range(ends)])  5.61 us
    gather x1, local copies, waits for them, and re-layouts, shards(): partner = jnp.take(stacked, picked, axis=1)  3.9 us
  transfers between devices with their start and end apart: 8, of which 4 were waited for; matrix products, arithmetic and copies ran while one was open for 7% of the time, Pallas kernels for 0%

commit v1 on v0

v1 whole, which is shorter than its diff:
```python
import functools

import jax
import jax.numpy as jnp
from jax import lax
from jax.experimental import pallas as pl
from jax.experimental.pallas import tpu as pltpu
from jax.sharding import PartitionSpec as P

SLOTS = 4
DATES = 32
MAPS = 3 * SLOTS + 1
GROUPS = 2 * MAPS
HALO_LANE = 32

epsilon = 1e-06


def three_parts(value):
    high = value.astype(jnp.bfloat16)
    rest = value - high.astype(jnp.float32)
    middle = rest.astype(jnp.bfloat16)
    low = (rest - middle.astype(jnp.float32)).astype(jnp.bfloat16)
    return high, middle, low


def looks_kernel(offs_smem, offs_ref, tiles_ref, looks_ref, edge_ref, prod, power, stack):
    half = lax.rem(lax.axis_index("date"), 2)

    def powers(d, carry):
        for t in range(2):
            real = tiles_ref[d, 0, t]
            imag = tiles_ref[d, 1, t]
            value = real * real + imag * imag
            power[t, d] = value
            prod[t, MAPS - 1, pl.ds(pl.multiple_of(d * 8, 8), 8), :] = value
        return carry

    lax.fori_loop(0, DATES, powers, 0, unroll=4)

    def pairs(d, carry):
        rows = pl.ds(pl.multiple_of(d * 8, 8), 8)
        for t in range(2):
            master_real = tiles_ref[d, 0, t]
            master_imag = tiles_ref[d, 1, t]
            for j in range(SLOTS):
                p = jnp.minimum(d + offs_smem[d * SLOTS + j], DATES - 1)
                partner_real = tiles_ref[p, 0, t]
                partner_imag = tiles_ref[p, 1, t]
                prod[t, j, rows, :] = master_real * partner_real + master_imag * partner_imag
                prod[t, SLOTS + j, rows, :] = master_imag * partner_real - master_real * partner_imag
                prod[t, 2 * SLOTS + j, rows, :] = power[t, p]
        return carry

    lax.fori_loop(0, DATES, pairs, 0, unroll=2)

    live = (offs_ref[...] > 0).astype(jnp.float32) / 64.0
    lives = [jnp.broadcast_to(live[:, j : j + 1], (DATES, 128)) for j in range(SLOTS)]
    for m in range(MAPS):
        scale = lives[m % SLOTS] if m < MAPS - 1 else 1.0 / 64.0
        for r in range(2):
            g = 2 * m + r
            for t in range(2):
                total = prod[t, m, pl.ds(4 * r, DATES, stride=8), :]
                for i in range(1, 4):
                    total = total + prod[t, m, pl.ds(4 * r + i, DATES, stride=8), :]
                for q, part in enumerate(three_parts(total * scale)):
                    lanes = 128 * (3 * t + q)
                    stack[pl.ds(DATES * g, DATES), lanes : lanes + 128] = part

    lane = lax.broadcasted_iota(jnp.int32, (768, 256), 0)
    place = lax.broadcasted_iota(jnp.int32, (768, 256), 1)
    look = (lane // 384) * 8 + (lane % 128) // 16
    want = jnp.where(place < 128, place % 16, half * 15)
    sums = (look == want).astype(jnp.bfloat16)
    out = jnp.dot(stack[...], sums, preferred_element_type=jnp.float32)
    lanes = lax.broadcasted_iota(jnp.int32, (DATES, 128), 1)
    edge = jnp.zeros((DATES, 128), jnp.float32)
    for k in range(4):
        block = jnp.zeros((DATES, 128), jnp.float32)
        for g in range(8 * k, min(8 * k + 8, GROUPS)):
            rows = slice(DATES * g, DATES * g + DATES)
            block = jnp.where(lanes // 16 == g - 8 * k, out[rows, :128], block)
            edge = jnp.where(lanes == HALO_LANE + g, out[rows, 128:], edge)
        looks_ref[pl.ds(k, DATES, stride=4), :] = block
    edge_ref[...] = edge


def local_looks(offsets, tiles):
    vmem = pl.BlockSpec(memory_space=pltpu.VMEM)
    return pl.pallas_call(
        looks_kernel,
        out_shape=(
            jax.ShapeDtypeStruct((4 * DATES, 128), jnp.float32),
            jax.ShapeDtypeStruct((DATES, 128), jnp.float32),
        ),
        in_specs=[pl.BlockSpec(memory_space=pltpu.SMEM), vmem, vmem],
        out_specs=(vmem, vmem),
        scratch_shapes=[
            pltpu.VMEM((2, MAPS, 8 * DATES, 128), jnp.float32),
            pltpu.VMEM((2, DATES, 8, 128), jnp.float32),
            pltpu.VMEM((GROUPS * DATES, 768), jnp.bfloat16),
        ],
        name="looks",
    )(offsets.reshape(-1), offsets, tiles)


def with_edge_kernel(looks_ref, edge_ref, out_ref):
    rows = pl.ds(3, DATES, stride=4)
    out_ref[...] = looks_ref[...]
    out_ref[rows, :] = looks_ref[rows, :] + edge_ref[...]


def with_edge(looks, edge):
    vmem = pl.BlockSpec(memory_space=pltpu.VMEM)
    return pl.pallas_call(
        with_edge_kernel,
        out_shape=jax.ShapeDtypeStruct((4 * DATES, 128), jnp.float32),
        in_specs=[vmem, vmem],
        out_specs=vmem,
        name="with_edge",
    )(looks, edge)


def finish_kernel(offs_smem, looks_ref, inter_ref, coh_ref):
    date = lax.axis_index("date")
    lanes = lax.broadcasted_iota(jnp.int32, (16, 128), 1)
    blocks = [[looks_ref[pl.ds(4 * half + k, 16, stride=8), :] for k in range(4)] for half in range(2)]

    def cells(m, r):
        g = 2 * m + r
        k, at = g // 8, 16 * (g % 8)
        value = jnp.zeros((16, 128), jnp.float32)
        for half in range(2):
            piece = pltpu.roll(blocks[half][k], (16 * half - at) % 128, 1)
            value = jnp.where(lanes // 16 == half, piece, value)
        left = pltpu.roll(blocks[0][3], (127 - HALO_LANE - g) % 128, 1)
        right = pltpu.roll(blocks[1][3], (32 - HALO_LANE - g) % 128, 1)
        return jnp.where(lanes == 127, left, jnp.where(lanes == 32, right, value))

    row = lax.broadcasted_iota(jnp.int32, (16, 128), 0)

    def window(m):
        across = []
        for r in range(2):
            value = cells(m, r)
            if m < 2 * SLOTS:
                inter_ref[m // SLOTS, 0, m % SLOTS, pl.ds(r, 16, stride=2), :] = value[:, :32]
            across.append(value + pltpu.roll(value, 1, 1) + pltpu.roll(value, 127, 1))
        both = across[0] + across[1]
        above = jnp.where(row == 0, 0.0, pltpu.roll(across[1], 1, 0))
        below = jnp.where(row == 15, 0.0, pltpu.roll(across[0], 15, 0))
        return both + above, both + below

    own = window(MAPS - 1)
    for j in range(SLOTS):
        live = (offs_smem[date * SLOTS + j] > 0).astype(jnp.float32)
        real, imag, partner = window(j), window(SLOTS + j), window(2 * SLOTS + j)
        for r in range(2):
            magnitude = jnp.sqrt(real[r] * real[r] + imag[r] * imag[r])
            value = magnitude / (jnp.sqrt((own[r] * live) * partner[r]) + epsilon)
            coh_ref[0, j, pl.ds(r, 16, stride=2), :] = value[:, :32]


def finish(offsets, looks):
    vmem = pl.BlockSpec(memory_space=pltpu.VMEM)
    return pl.pallas_call(
        finish_kernel,
        out_shape=(
            jax.ShapeDtypeStruct((2, 1, SLOTS, 32, 32), jnp.float32),
            jax.ShapeDtypeStruct((1, SLOTS, 32, 32), jnp.float32),
        ),
        in_specs=[pl.BlockSpec(memory_space=pltpu.SMEM), vmem],
        out_specs=(vmem, vmem),
        name="finish",
    )(offsets.reshape(-1), looks)


def edge_pairs(dates, cols):
    pairs = []
    for block in range(dates // 2):
        for c in range(1, cols):
            here, there = 2 * block * cols + c, (2 * block + 1) * cols + c - 1
            pairs += [(here, there), (there, here)]
    return pairs


def shards(slc, offsets):
    tiles = slc.reshape(2, 16, 8, 2, 2, 128).transpose(1, 3, 0, 4, 2, 5).reshape(DATES, 2, 2, 8, 128)
    tiles = lax.all_to_all(tiles, "date", 0, 0, tiled=True)
    looks, edge = local_looks(offsets, tiles)
    edge = lax.ppermute(edge, ("date", "col"), edge_pairs(DATES, lax.axis_size("col")))
    looks = with_edge(looks, edge)
    looks = lax.all_to_all(looks.reshape(DATES, 4, 128), "date", 0, 0, tiled=True)
    return finish(offsets, looks.reshape(4 * DATES, 128))


def solution(mesh):
    placed = (P(None, "date", None, "col"), P())
    return jax.shard_map(
        shards,
        mesh=mesh,
        in_specs=placed,
        out_specs=(P(None, "date", None, None, "col"), P("date", None, None, "col")),
        check_vma=False,
    )
```

time: 187 us -> 65.1 us (0.35)
  the two profiles are of different devices: /device:TPU:31 before, /device:TPU:32 now
where the time goes in v1:
time: 65.1 us; the launch traced here: 64.6 us
  waiting for transfers between devices  21.4 us (33%)
  blocking collectives  15.7 us (24%)
  starting transfers between devices  15.2 us (23%)
  Pallas kernels  7.67 us (12%)
  local copies, waits for them, and re-layouts  4.05 us (6%)
  between operations  0.66 us (1%)
    all_to_all x1, waiting for transfers between devices, shards(): tiles = lax.all_to_all(tiles, 'date', 0, 0, tiled=True)  15.9 us
    all_to_all x1, blocking collectives, shards(): lax.all_to_all(looks.reshape(DATES, 4, 128), 'date', 0, 0, tiled=True)  15.7 us
    all_to_all x1, starting transfers between devices, shards(): tiles = lax.all_to_all(tiles, 'date', 0, 0, tiled=True)  13.3 us
    ppermute x1, waiting for transfers between devices, shards(): lax.ppermute(edge, ('date', 'col'), edge_pairs(DATES, lax.axis_size('col')))  5.45 us
    pallas_call x1, Pallas kernels, local_looks(): pl.pallas_call(looks_kernel, out_shape=(jax.ShapeDtypeStruct((4 * DATES,...  3.5 us
    pallas_call x1, Pallas kernels, finish(): pl.pallas_call(finish_kernel, out_shape=(jax.ShapeDtypeStruct((2, 1, SLOT...  2.7 us
    ppermute x1, starting transfers between devices, shards(): lax.ppermute(edge, ('date', 'col'), edge_pairs(DATES, lax.axis_size('col')))  1.91 us
    reshape x1, local copies, waits for them, and re-layouts, shards(): slc.reshape(2, 16, 8, 2, 2, 128).transpose(1, 3, 0, 4, 2, 5)  1.9 us
  transfers between devices with their start and end apart: 2, of which 2 were waited for; matrix products, arithmetic and copies ran while one was open for 1% of the time, Pallas kernels for 0%

profile of v1, /device:TPU:32, one launch (start us, length us, event | category | flops | bytes accessed | tf_op | source)
XLA Modules:
  0.0 64.6 jit_solution(9105642535227882809)
XLA Ops:
  0.6 1.9 %copy.8 = f32[2,16,8,2,2,128]{5,2,4,0,3,1:T(8,128)} copy(f32[2,16,8,2,2,128]{5,2,4,3,1,0:T(8,128)} %bitcast.6) | data formatting | bytes 1048576 | tf_op jit(solution)/shard_map/reshape | solution.py:189
  2.5 0.0 copy-start.3
  2.5 13.3 %all-to-all-start = ((f32[32,2,2,8,128]{4,3,2,1,0:T(8,128)}), f32[32,2,2,8,128]{4,3,2,1,0:T(8,128)S(1)}, u32[]{:S(2)}, u32[]{:S(2)}) async-start(f32[32,2,2,8,128]{4,3,2,1,0:T(8,128)} %bitcast.2), calls=%async_computation | async-start | bytes 1048576 | tf_op jit(solution)/shard_map/all_to_all | solution.py:190
  15.8 0.0 copy-done.3
  15.8 0.1 copy.7.offs_ref
  15.9 0.0 copy-start.1
  15.9 0.7 %reshape.20.offs_smem = s32[128]{0:T(128)} reshape(s32[32,4]{1,0:T(8,128)S(1)} %copy.7.offs_ref) | data formatting | bytes 1024 | tf_op jit(solution)/shard_map/reshape | solution.py:176
  16.6 15.9 %all-to-all-done.tiles_ref = f32[32,2,2,8,128]{4,3,2,1,0:T(8,128)S(1)} async-done(((f32[32,2,2,8,128]{4,3,2,1,0:T(8,128)}), f32[32,2,2,8,128]{4,3,2,1,0:T(8,128)S(1)}, u32[]{:S(2)}, u32[]{:S(2)}) %all-to-all-start) | async-done | bytes 524320 | tf_op jit(solution)/shard_map/all_to_all | solution.py:190
  32.5 0.0 copy-done.1
  32.5 0.0 copy-start
  32.5 0.8 %copy-done = f32[32,2,2,8,128]{4,3,2,1,0:T(8,128)} copy-done((f32[32,2,2,8,128]{4,3,2,1,0:T(8,128)}, f32[32,2,2,8,128]{4,3,2,1,0:T(8,128)S(1)}, u32[]{:S(2)}) %copy-start) | copy-done | bytes 524312
  33.3 3.5 %looks.1 = (f32[128,128]{1,0:T(8,128)}, f32[32,128]{1,0:T(8,128)}) custom-call(s32[128]{0:T(128)} %reshape.20.offs_smem, s32[32,4]{1,0:T(8,128)} %copy-done.1, f32[32,2,2,8,128]{4,3,2,1,0:T(8,128)} %copy-done), custom_call_target="tpu_custom_call" | custom-call | tf_op jit(solution)/shard_map/looks/pallas_call | solution.py:91
  36.8 1.9 %collective-permute-start = (f32[32,128]{1,0:T(8,128)}, f32[32,128]{1,0:T(8,128)S(1)}, u32[]{:S(2)}, u32[]{:S(2)}) collective-permute-start(f32[32,128]{1,0:T(8,128)} %get-tuple-element.5), channel_id=1, source_target_pairs={{1,16},{16,1},{2,17},{17,2},{3,18},{18,3},{4,19},{19,4},{5,20},{20... | collective-permute-start | bytes 49160 | tf_op jit(solution)/shard_map/ppermute | solution.py:192
  38.7 5.4 %collective-permute-done.edge_ref = f32[32,128]{1,0:T(8,128)S(1)} collective-permute-done((f32[32,128]{1,0:T(8,128)}, f32[32,128]{1,0:T(8,128)S(1)}, u32[]{:S(2)}, u32[]{:S(2)}) %collective-permute-start) | collective-permute-done | bytes 16416 | tf_op jit(solution)/shard_map/ppermute | solution.py:192
  44.2 0.0 copy-start.2
  44.2 0.6 copy-done.2
  44.8 1.5 %with_edge.1 = f32[128,128]{1,0:T(8,128)} custom-call(f32[128,128]{1,0:T(8,128)} %get-tuple-element.4.looks_ref, f32[32,128]{1,0:T(8,128)} %copy-done.2), custom_call_target="tpu_custom_call" | custom-call | tf_op jit(solution)/shard_map/with_edge/pallas_call | solution.py:116
  46.3 15.7 %all_to_all.10 = f32[32,4,128]{2,1,0:T(4,128)} all-to-all(f32[32,4,128]{2,1,0:T(4,128)} %bitcast.8), channel_id=1, replica_groups=mesh['date'=32,'col'=16] {'date'}, dimensions={0} | all-to-all | bytes 131072 | tf_op jit(solution)/shard_map/all_to_all | solution.py:194
  61.9 2.7 %finish.1 = (f32[2,1,4,32,32]{4,3,2,1,0:T(8,128)}, f32[1,4,32,32]{3,2,1,0:T(8,128)}) custom-call(s32[128]{0:T(128)} %reshape.20.offs_smem, f32[128,128]{1,0:T(8,128)} %bitcast.7), custom_call_target="tpu_custom_call" | custom-call | tf_op jit(solution)/shard_map/finish/pallas_call | solution.py:167
Async XLA Ops:
  2.5 13.3 %copy-start.3 = (s32[32,4]{0,1:T(4,128)S(1)}, s32[32,4]{0,1:T(4,128)}, u32[]{:S(2)}) copy-start(s32[32,4]{0,1:T(4,128)} %param.3) | copy-start | bytes 1540
  2.5 30.0 %all-to-all-start = ((f32[32,2,2,8,128]{4,3,2,1,0:T(8,128)}), f32[32,2,2,8,128]{4,3,2,1,0:T(8,128)S(1)}, u32[]{:S(2)}, u32[]{:S(2)}) async-start(f32[32,2,2,8,128]{4,3,2,1,0:T(8,128)} %bitcast.2), calls=%async_computation | async-start | bytes 1048576 | tf_op jit(solution)/shard_map/all_to_all | solution.py:190
  15.9 16.6 %copy-start.1 = (s32[32,4]{1,0:T(8,128)}, s32[32,4]{1,0:T(8,128)S(1)}, u32[]{:S(2)}) copy-start(s32[32,4]{1,0:T(8,128)S(1)} %copy.7.offs_ref) | copy-start | bytes 1540
  32.5 0.8 %copy-start = (f32[32,2,2,8,128]{4,3,2,1,0:T(8,128)}, f32[32,2,2,8,128]{4,3,2,1,0:T(8,128)S(1)}, u32[]{:S(2)}) copy-start(f32[32,2,2,8,128]{4,3,2,1,0:T(8,128)S(1)} %all-to-all-done.tiles_ref) | copy-start | bytes 1572868
  36.8 7.4 %collective-permute-start = (f32[32,128]{1,0:T(8,128)}, f32[32,128]{1,0:T(8,128)S(1)}, u32[]{:S(2)}, u32[]{:S(2)}) collective-permute-start(f32[32,128]{1,0:T(8,128)} %get-tuple-element.5), channel_id=1, source_target_pairs={{1,16},{16,1},{2,17},{17,2},{3,18},{18,3},{4,19},{19,4},{5,20},{20... | collective-permute-start | bytes 49160 | tf_op jit(solution)/shard_map/ppermute | solution.py:192
  44.2 0.6 copy-start.2

commit v2 on v1

v2 whole, which is shorter than its diff:
```python
import jax
import jax.numpy as jnp
from jax import lax
from jax.experimental import pallas as pl
from jax.experimental.pallas import tpu as pltpu
from jax.sharding import PartitionSpec as P

SLOTS = 4
DATES = 32
MAX_OFFSET = 6
MAPS = 3 * SLOTS + 1
GROUPS = 2 * MAPS
HALO_LANE = 32
STAGES = 4

epsilon = 1e-06

VMEM = pl.BlockSpec(memory_space=pltpu.VMEM)
ANY = pl.BlockSpec(memory_space=pl.ANY)


def in_vmem(value):
    return pltpu.with_memory_space_constraint(value, pltpu.VMEM)


def odd_col():
    return lax.rem(lax.axis_index("col"), 2)


def own_half():
    return lax.rem(lax.axis_index("date") + lax.axis_index("col"), 2)


def two_parts(value):
    high = value.astype(jnp.bfloat16)
    return high, (value - high.astype(jnp.float32)).astype(jnp.bfloat16)


def pieces_kernel(slc_ref, out_ref, sems):
    odd = odd_col()
    copies = [
        pltpu.make_async_copy(
            slc_ref.at[p, :, half],
            out_ref.at[:, jnp.bitwise_xor(odd, half), p],
            sems.at[p, half],
        )
        for p in range(2)
        for half in range(2)
    ]
    for copy in copies:
        copy.start()
    for copy in copies:
        copy.wait()


def pieces(slc):
    tiles = slc.reshape(2, 16, 8, 2, 2, 128).transpose(0, 1, 3, 4, 2, 5)
    return pl.pallas_call(
        pieces_kernel,
        out_shape=pltpu.VMEM((16, 2, 2, 2, 8, 128), jnp.float32),
        in_specs=[ANY],
        out_specs=VMEM,
        scratch_shapes=[pltpu.SemaphoreType.DMA((2, 2))],
        name="pieces",
    )(tiles)


def edge_kernel(offs_ref, tiles_ref, edge_ref, shifted, stack):
    half = own_half()
    lanes = lax.broadcasted_iota(jnp.int32, (DATES, 128), 1)
    packed = []
    for p in range(2):
        value = jnp.zeros((DATES, 128), jnp.float32)
        for i in range(8):
            row = tiles_ref[pl.ds(16 * p + 8 * half + i, DATES, stride=32), :]
            value = jnp.where(lanes // 16 == i, pltpu.roll(row, 16 * (half + i), 1), value)
        packed.append(value)
    packed.append(packed[0] * packed[0] + packed[1] * packed[1])
    for q in range(3):
        shifted[q, 0:DATES, :] = packed[q]
        shifted[q, DATES : DATES + 8, :] = jnp.zeros((8, 128), jnp.float32)
    offs = offs_ref[...]
    looks = [None] * (MAPS - 1) + [packed[2]]
    for j in range(SLOTS):
        offset = jnp.broadcast_to(offs[:, j : j + 1], (DATES, 128))
        partner = [jnp.zeros((DATES, 128), jnp.float32)] * 3
        for step in range(1, MAX_OFFSET + 1):
            partner = [jnp.where(offset == step, shifted[q, step : step + DATES, :], partner[q]) for q in range(3)]
        looks[j] = packed[0] * partner[0] + packed[1] * partner[1]
        looks[SLOTS + j] = packed[1] * partner[0] - packed[0] * partner[1]
        looks[2 * SLOTS + j] = partner[2]
    for m in range(MAPS):
        for q, part in enumerate(two_parts(looks[m] / 64.0)):
            stack[DATES * m : DATES * m + DATES, 128 * q : 128 * q + 128] = part
    lane = lax.broadcasted_iota(jnp.int32, (256, 128), 0)
    place = lax.broadcasted_iota(jnp.int32, (256, 128), 1)
    sums = ((lane % 128) // 64 == place % 2).astype(jnp.bfloat16)
    out = jnp.dot(stack[...], sums, preferred_element_type=jnp.float32)
    edge = jnp.zeros((DATES, 128), jnp.float32)
    for m in range(MAPS):
        edge = jnp.where((lanes - HALO_LANE) // 2 == m, out[DATES * m : DATES * m + DATES, :], edge)
    edge_ref[...] = jnp.where(lanes >= HALO_LANE, edge, 0.0)


def edge_looks(offsets, tiles):
    return pl.pallas_call(
        edge_kernel,
        out_shape=pltpu.VMEM((DATES, 128), jnp.float32),
        in_specs=[VMEM, VMEM],
        out_specs=VMEM,
        scratch_shapes=[
            pltpu.VMEM((3, DATES + 8, 128), jnp.float32),
            pltpu.VMEM((MAPS * DATES, 256), jnp.bfloat16),
        ],
        name="edge_looks",
    )(in_vmem(offsets), in_vmem(tiles))


def looks_kernel(offs_smem, offs_ref, tiles_ref, looks_ref, prod, power, stack):
    def tile(d, p, t):
        return tiles_ref[pl.ds(pl.multiple_of(d * 32 + 16 * p + 8 * t, 8), 8), :]

    def powers(d, carry):
        for t in range(2):
            real, imag = tile(d, 0, t), tile(d, 1, t)
            value = real * real + imag * imag
            power[t, d] = value
            prod[t, MAPS - 1, pl.ds(pl.multiple_of(d * 8, 8), 8), :] = value
        return carry

    lax.fori_loop(0, DATES, powers, 0, unroll=4)

    def pairs(d, carry):
        rows = pl.ds(pl.multiple_of(d * 8, 8), 8)
        for t in range(2):
            master_real, master_imag = tile(d, 0, t), tile(d, 1, t)
            for j in range(SLOTS):
                p = jnp.minimum(d + offs_smem[d, j], DATES - 1)
                partner_real, partner_imag = tile(p, 0, t), tile(p, 1, t)
                prod[t, j, rows, :] = master_real * partner_real + master_imag * partner_imag
                prod[t, SLOTS + j, rows, :] = master_imag * partner_real - master_real * partner_imag
                prod[t, 2 * SLOTS + j, rows, :] = power[t, p]
        return carry

    lax.fori_loop(0, DATES, pairs, 0, unroll=2)

    live = (offs_ref[...] > 0).astype(jnp.float32) / 64.0
    lives = [jnp.broadcast_to(live[:, j : j + 1], (DATES, 128)) for j in range(SLOTS)]
    for m in range(MAPS):
        scale = lives[m % SLOTS] if m < MAPS - 1 else 1.0 / 64.0
        for r in range(2):
            g = 2 * m + r
            for t in range(2):
                total = prod[t, m, pl.ds(4 * r, DATES, stride=8), :]
                for i in range(1, 4):
                    total = total + prod[t, m, pl.ds(4 * r + i, DATES, stride=8), :]
                for q, part in enumerate(two_parts(total * scale)):
                    lanes = 128 * (2 * t + q)
                    stack[pl.ds(DATES * g, DATES), lanes : lanes + 128] = part

    lane = lax.broadcasted_iota(jnp.int32, (512, 128), 0)
    place = lax.broadcasted_iota(jnp.int32, (512, 128), 1)
    sums = ((lane // 256) * 8 + (lane % 128) // 16 == place % 16).astype(jnp.bfloat16)
    out = jnp.dot(stack[...], sums, preferred_element_type=jnp.float32)
    lanes = lax.broadcasted_iota(jnp.int32, (DATES, 128), 1)
    for k in range(4):
        block = jnp.zeros((DATES, 128), jnp.float32)
        for g in range(8 * k, min(8 * k + 8, GROUPS)):
            block = jnp.where(lanes // 16 == g - 8 * k, out[DATES * g : DATES * g + DATES, :], block)
        looks_ref[pl.ds(k, DATES, stride=4), :] = block


def local_looks(offsets, tiles):
    return pl.pallas_call(
        looks_kernel,
        out_shape=pltpu.VMEM((4 * DATES, 128), jnp.float32),
        in_specs=[pl.BlockSpec(memory_space=pltpu.SMEM), VMEM, VMEM],
        out_specs=VMEM,
        scratch_shapes=[
            pltpu.VMEM((2, MAPS, 8 * DATES, 128), jnp.float32),
            pltpu.VMEM((2, DATES, 8, 128), jnp.float32),
            pltpu.VMEM((GROUPS * DATES, 512), jnp.bfloat16),
        ],
        name="looks",
    )(offsets, in_vmem(offsets), in_vmem(tiles))


def with_edge_kernel(looks_ref, edge_ref, out_ref):
    rows = pl.ds(3, DATES, stride=4)
    out_ref[rows, :] = looks_ref[rows, :] + edge_ref[...]


def with_edge(looks, edge):
    return pl.pallas_call(
        with_edge_kernel,
        out_shape=pltpu.VMEM((4 * DATES, 128), jnp.float32),
        in_specs=[VMEM, VMEM],
        out_specs=VMEM,
        input_output_aliases={0: 0},
        name="with_edge",
    )(in_vmem(looks), in_vmem(edge))


def finish_kernel(offs_ref, looks_ref, inter_ref, coh_ref):
    odd = odd_col()
    lanes = lax.broadcasted_iota(jnp.int32, (16, 128), 1)
    blocks = [
        [looks_ref[pl.ds(4 * jnp.bitwise_xor(odd, half) + k, 16, stride=8), :] for k in range(4)]
        for half in range(2)
    ]

    def cells(m, r):
        g = 2 * m + r
        k, at = g // 8, 16 * (g % 8)
        value = jnp.zeros((16, 128), jnp.float32)
        for half in range(2):
            piece = pltpu.roll(blocks[half][k], (16 * half - at) % 128, 1)
            value = jnp.where(lanes // 16 == half, piece, value)
        left = pltpu.roll(blocks[0][3], (127 - HALO_LANE - g) % 128, 1)
        right = pltpu.roll(blocks[1][3], (32 - HALO_LANE - g) % 128, 1)
        return jnp.where(lanes == 127, left, jnp.where(lanes == 32, right, value))

    row = lax.broadcasted_iota(jnp.int32, (16, 128), 0)

    def window(m):
        across = []
        for r in range(2):
            value = cells(m, r)
            if m < 2 * SLOTS:
                inter_ref[m // SLOTS, 0, m % SLOTS, pl.ds(r, 16, stride=2), :] = value[:, :32]
            across.append(value + pltpu.roll(value, 1, 1) + pltpu.roll(value, 127, 1))
        both = across[0] + across[1]
        above = jnp.where(row == 0, 0.0, pltpu.roll(across[1], 1, 0))
        below = jnp.where(row == 15, 0.0, pltpu.roll(across[0], 15, 0))
        return both + above, both + below

    own = window(MAPS - 1)
    lives = (offs_ref[pl.ds(lax.axis_index("date"), 1), :] > 0).astype(jnp.float32)
    for j in range(SLOTS):
        live = jnp.broadcast_to(lives[:, j : j + 1], (16, 128))
        real, imag, partner = window(j), window(SLOTS + j), window(2 * SLOTS + j)
        for r in range(2):
            magnitude = jnp.sqrt(real[r] * real[r] + imag[r] * imag[r])
            value = magnitude / (jnp.sqrt((own[r] * live) * partner[r]) + epsilon)
            coh_ref[0, j, pl.ds(r, 16, stride=2), :] = value[:, :32]


def finish(offsets, looks):
    return pl.pallas_call(
        finish_kernel,
        out_shape=(
            jax.ShapeDtypeStruct((2, 1, SLOTS, 32, 32), jnp.float32),
            jax.ShapeDtypeStruct((1, SLOTS, 32, 32), jnp.float32),
        ),
        in_specs=[VMEM, VMEM],
        out_specs=(VMEM, VMEM),
        name="finish",
    )(in_vmem(offsets), in_vmem(looks))


def edge_pairs(dates, cols):
    pairs = []
    for c in range(1, cols):
        for d in range(c % 2, dates, 2):
            here, there = d * cols + c, d * cols + c - 1
            pairs += [(here, there), (there, here)]
    return pairs


def shards(slc, offsets):
    tiles, offsets = lax.optimization_barrier((pieces(slc).reshape(DATES, 32, 128), offsets))
    tiles = lax.all_to_all(tiles, "date", 0, 0, tiled=True)
    tiles = tiles.reshape(32 * DATES, 128)
    edge = edge_looks(offsets, tiles)
    edge = lax.ppermute(edge, ("date", "col"), edge_pairs(DATES, lax.axis_size("col")))
    looks = with_edge(local_looks(offsets, tiles), edge)
    looks = lax.all_to_all(looks.reshape(DATES, 4, 128), "date", 0, 0, tiled=True)
    return finish(offsets, looks.reshape(4 * DATES, 128))


def solution(mesh):
    placed = (P(None, "date", None, "col"), P())
    return jax.shard_map(
        shards,
        mesh=mesh,
        in_specs=placed,
        out_specs=(P(None, "date", None, None, "col"), P("date", None, None, "col")),
        check_vma=False,
    )
```

time: 65.1 us -> 56.8 us (0.87)
  local copies, waits for them, and re-layouts: 4.05 us -> 0.09 us
  waiting for transfers between devices: 21.4 us -> 18.5 us
  Pallas kernels: 7.67 us -> 6.7 us
    ppermute x1, waiting for transfers between devices: 5.45 us -> 1.91 us  [shards(): lax.ppermute(edge, ('date', 'col'), edge_pairs(DATES, lax.axis_size('col')))]
    reshape x2 -> x0, local copies, waits for them, and re-layouts: 2.57 us -> none  [the longest x1 1.9 us: shards(): slc.reshape(2, 16, 8, 2, 2, 128).transpose(1, 3, 0, 4, 2, 5)]
    unnamed x9 -> x2, local copies, waits for them, and re-layouts: 1.48 us -> 0.01 us
    pallas_call x1, Pallas kernels: 2.7 us -> 1.85 us  [finish(): pl.pallas_call(finish_kernel, out_shape=(jax.ShapeDtypeStruct((2, 1, SLOT...]
    all_to_all x1, waiting for transfers between devices: 15.9 us -> 16.6 us  [shards(): tiles = lax.all_to_all(tiles, 'date', 0, 0, tiled=True)]
    pallas_call x2 -> x4, Pallas kernels: 4.98 us -> 4.85 us  [the longest x1 2.43 us: local_looks(): pl.pallas_call(looks_kernel, out_shape=pltpu.VMEM((4 * DATES, 128), jnp.f...]
  transfers between devices with their start and end apart: 2 -> 2, of which waited for: 2 -> 2; matrix products, arithmetic and copies ran while one was open for 1% -> 0% of each run, Pallas kernels for 0% -> 4%
where the time goes in v2:
time: 56.8 us; the launch traced here: 56.5 us
  waiting for transfers between devices  18.5 us (33%)
  blocking collectives  15.4 us (27%)
  starting transfers between devices  15.1 us (27%)
  Pallas kernels  6.7 us (12%)
  between operations  0.69 us (1%)
    all_to_all x1, waiting for transfers between devices, shards(): tiles = lax.all_to_all(tiles, 'date', 0, 0, tiled=True)  16.6 us
    all_to_all x1, blocking collectives, shards(): lax.all_to_all(looks.reshape(DATES, 4, 128), 'date', 0, 0, tiled=True)  15.4 us
    all_to_all x1, starting transfers between devices, shards(): tiles = lax.all_to_all(tiles, 'date', 0, 0, tiled=True)  13.2 us
    pallas_call x1, Pallas kernels, local_looks(): pl.pallas_call(looks_kernel, out_shape=pltpu.VMEM((4 * DATES, 128), jnp.f...  2.43 us
    pallas_call x1, Pallas kernels, pieces(): pl.pallas_call(pieces_kernel, out_shape=pltpu.VMEM((16, 2, 2, 2, 8, 128),...  1.93 us
    ppermute x1, starting transfers between devices, shards(): lax.ppermute(edge, ('date', 'col'), edge_pairs(DATES, lax.axis_size('col')))  1.92 us
    ppermute x1, waiting for transfers between devices, shards(): lax.ppermute(edge, ('date', 'col'), edge_pairs(DATES, lax.axis_size('col')))  1.91 us
    pallas_call x1, Pallas kernels, finish(): pl.pallas_call(finish_kernel, out_shape=(jax.ShapeDtypeStruct((2, 1, SLOT...  1.85 us
  transfers between devices with their start and end apart: 2, of which 2 were waited for; matrix products, arithmetic and copies ran while one was open for 0% of the time, Pallas kernels for 4%

profile of v2, /device:TPU:32, one launch (start us, length us, event | category | flops | bytes accessed | tf_op | source)
XLA Modules:
  0.0 56.5 jit_solution(6173115398731931048)
XLA Ops:
  0.6 1.9 %pieces.1 = f32[16,2,2,2,8,128]{5,4,3,2,1,0:T(8,128)} custom-call(f32[2,16,2,2,8,128]{5,4,3,2,1,0:T(8,128)} %bitcast.11), custom_call_target="tpu_custom_call" | custom-call | tf_op jit(solution)/shard_map/pieces/pallas_call | solution.py:58
  2.6 0.0 copy-start
  2.6 13.2 %all-to-all-start = ((f32[32,32,128]{2,1,0:T(8,128)}), f32[32,32,128]{2,1,0:T(8,128)S(1)}, u32[]{:S(2)}, u32[]{:S(2)}) async-start(f32[32,32,128]{2,1,0:T(8,128)} %bitcast.2), calls=%async_computation | async-start | bytes 1048576 | tf_op jit(solution)/shard_map/all_to_all | solution.py:272
  15.8 0.0 copy-done
  15.8 0.1 copy.8.offs_smem.offs_ref
  15.9 16.6 %all-to-all-done = f32[32,32,128]{2,1,0:T(8,128)S(1)} async-done(((f32[32,32,128]{2,1,0:T(8,128)}), f32[32,32,128]{2,1,0:T(8,128)S(1)}, u32[]{:S(2)}, u32[]{:S(2)}) %all-to-all-start) | async-done | bytes 524320 | tf_op jit(solution)/shard_map/all_to_all | solution.py:272
  32.5 0.5 edge_looks.1
  33.0 1.9 %collective-permute-start = (f32[32,128]{1,0:T(8,128)S(1)}, f32[32,128]{1,0:T(8,128)S(1)}, u32[]{:S(2)}, u32[]{:S(2)}) collective-permute-start(f32[32,128]{1,0:T(8,128)S(1)} %edge_looks.1), channel_id=1, source_target_pairs={{17,16},{16,17},{49,48},{48,49},{81,80},{80,81},{113,112},{112,113... | collective-permute-start | bytes 49160 | tf_op jit(solution)/shard_map/ppermute | solution.py:275
  34.9 2.4 %looks.1.looks_ref = f32[128,128]{1,0:T(8,128)S(1)} custom-call(s32[32,4]{1,0:T(8,128)S(1)} %copy.8.offs_smem.offs_ref, s32[32,4]{1,0:T(8,128)S(1)} %copy.8.offs_smem.offs_ref, f32[1024,128]{1,0:T(8,128)S(1)} %bitcast.8), custom_call_target="tpu_custom_call" | custom-call | tf_op jit(solution)/shard_map/looks/pallas_call | solution.py:174
  37.3 1.9 %collective-permute-done.edge_ref = f32[32,128]{1,0:T(8,128)S(1)} collective-permute-done((f32[32,128]{1,0:T(8,128)S(1)}, f32[32,128]{1,0:T(8,128)S(1)}, u32[]{:S(2)}, u32[]{:S(2)}) %collective-permute-start) | collective-permute-done | bytes 16416 | tf_op jit(solution)/shard_map/ppermute | solution.py:275
  39.2 15.4 %all_to_all.10 = f32[32,4,128]{2,1,0:T(4,128)S(1)} all-to-all(f32[32,4,128]{2,1,0:T(4,128)S(1)} %bitcast.9), channel_id=1, replica_groups=mesh['date'=32,'col'=16] {'date'}, dimensions={0} | all-to-all | bytes 131072 | tf_op jit(solution)/shard_map/all_to_all | solution.py:277
  54.6 1.8 %finish.1 = (f32[2,1,4,32,32]{4,3,2,1,0:T(8,128)}, f32[1,4,32,32]{3,2,1,0:T(8,128)}) custom-call(s32[32,4]{1,0:T(8,128)S(1)} %copy.8.offs_smem.offs_ref, f32[128,128]{1,0:T(8,128)S(1)} %bitcast.10), custom_call_target="tpu_custom_call" | custom-call | tf_op jit(solution)/shard_map/finish/pallas_call | solution.py:249
  (1 shorter events, 0.0 us)
Async XLA Ops:
  2.6 13.2 %copy-start = (s32[32,4]{0,1:T(4,128)S(1)}, s32[32,4]{0,1:T(4,128)}, u32[]{:S(2)}) copy-start(s32[32,4]{0,1:T(4,128)} %param.3) | copy-start | bytes 1540
  2.6 29.9 %all-to-all-start = ((f32[32,32,128]{2,1,0:T(8,128)}), f32[32,32,128]{2,1,0:T(8,128)S(1)}, u32[]{:S(2)}, u32[]{:S(2)}) async-start(f32[32,32,128]{2,1,0:T(8,128)} %bitcast.2), calls=%async_computation | async-start | bytes 1048576 | tf_op jit(solution)/shard_map/all_to_all | solution.py:272
  33.0 6.3 %collective-permute-start = (f32[32,128]{1,0:T(8,128)S(1)}, f32[32,128]{1,0:T(8,128)S(1)}, u32[]{:S(2)}, u32[]{:S(2)}) collective-permute-start(f32[32,128]{1,0:T(8,128)S(1)} %edge_looks.1), channel_id=1, source_target_pairs={{17,16},{16,17},{49,48},{48,49},{81,80},{80,81},{113,112},{112,113... | collective-permute-start | bytes 49160 | tf_op jit(solution)/shard_map/ppermute | solution.py:275

commit v3 on v2

--- a/solution.py
+++ b/solution.py
@@ -11,7 +11,6 @@
 MAPS = 3 * SLOTS + 1
 GROUPS = 2 * MAPS
 HALO_LANE = 32
-STAGES = 4
 
 epsilon = 1e-06
 
@@ -36,8 +35,10 @@
     return high, (value - high.astype(jnp.float32)).astype(jnp.bfloat16)
 
 
-def pieces_kernel(slc_ref, out_ref, sems):
+def pieces_kernel(slc_ref, slots_ref, out_ref, offs_ref, slots, sems, slots_sem):
     odd = odd_col()
+    first = pltpu.make_async_copy(slots_ref, slots, slots_sem)
+    first.start()
     copies = [
         pltpu.make_async_copy(
             slc_ref.at[p, :, half],
@@ -49,20 +50,29 @@
     ]
     for copy in copies:
         copy.start()
+    first.wait()
+    offs_ref[...] = slots[...].T
     for copy in copies:
         copy.wait()
 
 
-def pieces(slc):
+def pieces(slc, offsets):
     tiles = slc.reshape(2, 16, 8, 2, 2, 128).transpose(0, 1, 3, 4, 2, 5)
     return pl.pallas_call(
         pieces_kernel,
-        out_shape=pltpu.VMEM((16, 2, 2, 2, 8, 128), jnp.float32),
-        in_specs=[ANY],
-        out_specs=VMEM,
-        scratch_shapes=[pltpu.SemaphoreType.DMA((2, 2))],
+        out_shape=(
+            pltpu.VMEM((16, 2, 2, 2, 8, 128), jnp.float32),
+            pltpu.VMEM((DATES, SLOTS), jnp.int32),
+        ),
+        in_specs=[ANY, ANY],
+        out_specs=(VMEM, VMEM),
+        scratch_shapes=[
+            pltpu.VMEM((SLOTS, DATES), jnp.int32),
+            pltpu.SemaphoreType.DMA((2, 2)),
+            pltpu.SemaphoreType.DMA,
+        ],
         name="pieces",
-    )(tiles)
+    )(tiles, offsets.T)
 
 
 def edge_kernel(offs_ref, tiles_ref, edge_ref, shifted, stack):
@@ -116,16 +126,14 @@
     )(in_vmem(offsets), in_vmem(tiles))
 
 
-def looks_kernel(offs_smem, offs_ref, tiles_ref, looks_ref, prod, power, stack):
+def looks_kernel(offs_smem, offs_ref, tiles_ref, looks_ref, prod, stack):
     def tile(d, p, t):
         return tiles_ref[pl.ds(pl.multiple_of(d * 32 + 16 * p + 8 * t, 8), 8), :]
 
     def powers(d, carry):
         for t in range(2):
             real, imag = tile(d, 0, t), tile(d, 1, t)
-            value = real * real + imag * imag
-            power[t, d] = value
-            prod[t, MAPS - 1, pl.ds(pl.multiple_of(d * 8, 8), 8), :] = value
+            prod[t, 2 * SLOTS, pl.ds(pl.multiple_of(d * 8, 8), 8), :] = real * real + imag * imag
         return carry
 
     lax.fori_loop(0, DATES, powers, 0, unroll=4)
@@ -139,15 +147,15 @@
                 partner_real, partner_imag = tile(p, 0, t), tile(p, 1, t)
                 prod[t, j, rows, :] = master_real * partner_real + master_imag * partner_imag
                 prod[t, SLOTS + j, rows, :] = master_imag * partner_real - master_real * partner_imag
-                prod[t, 2 * SLOTS + j, rows, :] = power[t, p]
         return carry
 
     lax.fori_loop(0, DATES, pairs, 0, unroll=2)
 
-    live = (offs_ref[...] > 0).astype(jnp.float32) / 64.0
+    offs = offs_ref[...]
+    live = (offs > 0).astype(jnp.float32) / 64.0
     lives = [jnp.broadcast_to(live[:, j : j + 1], (DATES, 128)) for j in range(SLOTS)]
-    for m in range(MAPS):
-        scale = lives[m % SLOTS] if m < MAPS - 1 else 1.0 / 64.0
+    for m in range(2 * SLOTS + 1):
+        scale = lives[m % SLOTS] if m < 2 * SLOTS else 1.0 / 64.0
         for r in range(2):
             g = 2 * m + r
             for t in range(2):
@@ -162,11 +170,30 @@
     place = lax.broadcasted_iota(jnp.int32, (512, 128), 1)
     sums = ((lane // 256) * 8 + (lane % 128) // 16 == place % 16).astype(jnp.bfloat16)
     out = jnp.dot(stack[...], sums, preferred_element_type=jnp.float32)
+    found = [out[DATES * g : DATES * g + DATES, :] for g in range(4 * SLOTS + 2)]
+
+    column = lax.broadcasted_iota(jnp.int32, (DATES, 2 * DATES), 1) % DATES
+    date = lax.broadcasted_iota(jnp.int32, (DATES, 2 * DATES), 0)
+    pick = []
+    for j in range(SLOTS):
+        offset = jnp.broadcast_to(offs[:, j : j + 1], (DATES, 2 * DATES))
+        pick.append(((column == date + offset) & (offset > 0)).astype(jnp.float32))
+    own = [jnp.concatenate(two_parts(value), axis=0) for value in found[4 * SLOTS :]]
+    partner = jnp.dot(
+        jnp.concatenate(pick, axis=0).astype(jnp.bfloat16),
+        jnp.concatenate(own, axis=1),
+        preferred_element_type=jnp.float32,
+    )
+    picked = [
+        partner[DATES * j : DATES * j + DATES, 128 * r : 128 * r + 128] for j in range(SLOTS) for r in range(2)
+    ]
+    found = found[: 4 * SLOTS] + picked + found[4 * SLOTS :]
+
     lanes = lax.broadcasted_iota(jnp.int32, (DATES, 128), 1)
     for k in range(4):
         block = jnp.zeros((DATES, 128), jnp.float32)
         for g in range(8 * k, min(8 * k + 8, GROUPS)):
-            block = jnp.where(lanes // 16 == g - 8 * k, out[DATES * g : DATES * g + DATES, :], block)
+            block = jnp.where(lanes // 16 == g - 8 * k, found[g], block)
         looks_ref[pl.ds(k, DATES, stride=4), :] = block
 
 
@@ -177,9 +204,8 @@
         in_specs=[pl.BlockSpec(memory_space=pltpu.SMEM), VMEM, VMEM],
         out_specs=VMEM,
         scratch_shapes=[
-            pltpu.VMEM((2, MAPS, 8 * DATES, 128), jnp.float32),
-            pltpu.VMEM((2, DATES, 8, 128), jnp.float32),
-            pltpu.VMEM((GROUPS * DATES, 512), jnp.bfloat16),
+            pltpu.VMEM((2, 2 * SLOTS + 1, 8 * DATES, 128), jnp.float32),
+            pltpu.VMEM(((4 * SLOTS + 2) * DATES, 512), jnp.bfloat16),
         ],
         name="looks",
     )(offsets, in_vmem(offsets), in_vmem(tiles))
@@ -201,7 +227,7 @@
     )(in_vmem(looks), in_vmem(edge))
 
 
-def finish_kernel(offs_ref, looks_ref, inter_ref, coh_ref):
+def finish_kernel(offs_ref, looks_ref, inter_out, coh_out, inter_ref, coh_ref, sems):
     odd = odd_col()
     lanes = lax.broadcasted_iota(jnp.int32, (16, 128), 1)
     blocks = [
@@ -234,15 +260,26 @@
         below = jnp.where(row == 15, 0.0, pltpu.roll(across[0], 15, 0))
         return both + above, both + below
 
+    copies = []
     own = window(MAPS - 1)
     lives = (offs_ref[pl.ds(lax.axis_index("date"), 1), :] > 0).astype(jnp.float32)
     for j in range(SLOTS):
         live = jnp.broadcast_to(lives[:, j : j + 1], (16, 128))
-        real, imag, partner = window(j), window(SLOTS + j), window(2 * SLOTS + j)
+        real, imag = window(j), window(SLOTS + j)
+        for p in range(2):
+            copy = pltpu.make_async_copy(inter_ref.at[p, 0, j], inter_out.at[p, 0, j], sems.at[p, j])
+            copy.start()
+            copies.append(copy)
+        partner = window(2 * SLOTS + j)
         for r in range(2):
             magnitude = jnp.sqrt(real[r] * real[r] + imag[r] * imag[r])
             value = magnitude / (jnp.sqrt((own[r] * live) * partner[r]) + epsilon)
             coh_ref[0, j, pl.ds(r, 16, stride=2), :] = value[:, :32]
+        last = pltpu.make_async_copy(coh_ref.at[0, j], coh_out.at[0, j], sems.at[2, j])
+        last.start()
+        copies.append(last)
+    for copy in copies:
+        copy.wait()
 
 
 def finish(offsets, looks):
@@ -253,7 +290,12 @@
             jax.ShapeDtypeStruct((1, SLOTS, 32, 32), jnp.float32),
         ),
         in_specs=[VMEM, VMEM],
-        out_specs=(VMEM, VMEM),
+        out_specs=(ANY, ANY),
+        scratch_shapes=[
+            pltpu.VMEM((2, 1, SLOTS, 32, 32), jnp.float32),
+            pltpu.VMEM((1, SLOTS, 32, 32), jnp.float32),
+            pltpu.SemaphoreType.DMA((3, SLOTS)),
+        ],
         name="finish",
     )(in_vmem(offsets), in_vmem(looks))
 
@@ -268,8 +310,8 @@
 
 
 def shards(slc, offsets):
-    tiles, offsets = lax.optimization_barrier((pieces(slc).reshape(DATES, 32, 128), offsets))
-    tiles = lax.all_to_all(tiles, "date", 0, 0, tiled=True)
+    tiles, offsets = pieces(slc, offsets)
+    tiles = lax.all_to_all(tiles.reshape(DATES, 32, 128), "date", 0, 0, tiled=True)
     tiles = tiles.reshape(32 * DATES, 128)
     edge = edge_looks(offsets, tiles)
     edge = lax.ppermute(edge, ("date", "col"), edge_pairs(DATES, lax.axis_size("col")))

time: 56.8 us -> 55.7 us (0.981)
  blocking collectives: 15.4 us -> 45 us
  waiting for transfers between devices: 18.5 us -> 2.13 us
  starting transfers between devices: 15.1 us -> 1.92 us
  Pallas kernels: 6.7 us -> 5.72 us
    all_to_all x0 -> x1, blocking collectives: none -> 29.7 us  [shards(): lax.all_to_all(tiles.reshape(DATES, 32, 128), 'date', 0, 0, tiled=True)]
    all_to_all x1 -> x0, waiting for transfers between devices: 16.6 us -> none  [shards(): tiles = lax.all_to_all(tiles, 'date', 0, 0, tiled=True)]
    all_to_all x1 -> x0, starting transfers between devices: 13.2 us -> none  [shards(): tiles = lax.all_to_all(tiles, 'date', 0, 0, tiled=True)]
    pallas_call x1, Pallas kernels: 1.93 us -> 1.15 us  [pieces(): pl.pallas_call(pieces_kernel, out_shape=(pltpu.VMEM((16, 2, 2, 2, 8, 128)...]
  transfers between devices with their start and end apart: 2 -> 1, of which waited for: 2 -> 1; matrix products, arithmetic and copies ran while one was open for 0% -> 0% of each run, Pallas kernels for 4% -> 4%
where the time goes in v3:
time: 55.7 us; the launch traced here: 55.4 us
  blocking collectives  45 us (81%)
  Pallas kernels  5.72 us (10%)
  waiting for transfers between devices  2.13 us (4%)
  starting transfers between devices  1.92 us (3%)
  between operations  0.66 us (1%)
    all_to_all x1, blocking collectives, shards(): lax.all_to_all(tiles.reshape(DATES, 32, 128), 'date', 0, 0, tiled=True)  29.7 us
    all_to_all x1, blocking collectives, shards(): lax.all_to_all(looks.reshape(DATES, 4, 128), 'date', 0, 0, tiled=True)  15.3 us
    pallas_call x1, Pallas kernels, local_looks(): pl.pallas_call(looks_kernel, out_shape=pltpu.VMEM((4 * DATES, 128), jnp.f...  2.21 us
    ppermute x1, waiting for transfers between devices, shards(): lax.ppermute(edge, ('date', 'col'), edge_pairs(DATES, lax.axis_size('col')))  2.13 us
    ppermute x1, starting transfers between devices, shards(): lax.ppermute(edge, ('date', 'col'), edge_pairs(DATES, lax.axis_size('col')))  1.92 us
    pallas_call x1, Pallas kernels, finish(): pl.pallas_call(finish_kernel, out_shape=(jax.ShapeDtypeStruct((2, 1, SLOT...  1.86 us
    pallas_call x1, Pallas kernels, pieces(): pl.pallas_call(pieces_kernel, out_shape=(pltpu.VMEM((16, 2, 2, 2, 8, 128)...  1.15 us
  transfers between devices with their start and end apart: 1, of which 1 were waited for; matrix products, arithmetic and copies ran while one was open for 0% of the time, Pallas kernels for 4%

profile of v3, /device:TPU:32, one launch (start us, length us, event | category | flops | bytes accessed | tf_op | source)
XLA Modules:
  0.0 55.4 jit_solution(7814980171501131396)
XLA Ops:
  0.6 1.2 %pieces.1 = (f32[16,2,2,2,8,128]{5,4,3,2,1,0:T(8,128)S(1)}, s32[32,4]{1,0:T(8,128)S(1)}) custom-call(f32[2,16,2,2,8,128]{5,4,3,2,1,0:T(8,128)} %bitcast.13, s32[4,32]{1,0:T(4,128)} %bitcast.14), custom_call_target="tpu_custom_call" | custom-call | tf_op jit(solution)/shard_map/pieces/pallas_call | solution.py:61
  1.8 29.7 %all_to_all.10 = f32[32,32,128]{2,1,0:T(8,128)S(1)} all-to-all(f32[32,32,128]{2,1,0:T(8,128)S(1)} %bitcast.11), channel_id=1, replica_groups=mesh['date'=32,'col'=16] {'date'}, dimensions={0} | all-to-all | bytes 1048576 | tf_op jit(solution)/shard_map/all_to_all | solution.py:314
  31.5 0.5 edge_looks.1
  32.0 1.9 %collective-permute-start = (f32[32,128]{1,0:T(8,128)S(1)}, f32[32,128]{1,0:T(8,128)S(1)}, u32[]{:S(2)}, u32[]{:S(2)}) collective-permute-start(f32[32,128]{1,0:T(8,128)S(1)} %edge_looks.1), channel_id=1, source_target_pairs={{17,16},{16,17},{49,48},{48,49},{81,80},{80,81},{113,112},{112,113... | collective-permute-start | bytes 49160 | tf_op jit(solution)/shard_map/ppermute | solution.py:317
  33.9 2.2 %looks.1.looks_ref = f32[128,128]{1,0:T(8,128)S(1)} custom-call(s32[32,4]{1,0:T(8,128)S(1)} %get-tuple-element.4.offs_smem.offs_ref, s32[32,4]{1,0:T(8,128)S(1)} %get-tuple-element.4.offs_smem.offs_ref, f32[1024,128]{1,0:T(8,128)S(1)} %bitcast.9), custom_call_target="tpu_custom_call" | custom-call | tf_op jit(solution)/shard_map/looks/pallas_call | solution.py:201
  36.1 2.1 %collective-permute-done.edge_ref = f32[32,128]{1,0:T(8,128)S(1)} collective-permute-done((f32[32,128]{1,0:T(8,128)S(1)}, f32[32,128]{1,0:T(8,128)S(1)}, u32[]{:S(2)}, u32[]{:S(2)}) %collective-permute-start) | collective-permute-done | bytes 16416 | tf_op jit(solution)/shard_map/ppermute | solution.py:317
  38.2 15.3 %all_to_all.11 = f32[32,4,128]{2,1,0:T(4,128)S(1)} all-to-all(f32[32,4,128]{2,1,0:T(4,128)S(1)} %bitcast.10), channel_id=1, replica_groups=mesh['date'=32,'col'=16] {'date'}, dimensions={0} | all-to-all | bytes 131072 | tf_op jit(solution)/shard_map/all_to_all | solution.py:319
  53.6 1.9 %finish.1 = (f32[2,1,4,32,32]{4,3,2,1,0:T(8,128)}, f32[1,4,32,32]{3,2,1,0:T(8,128)}) custom-call(s32[32,4]{1,0:T(8,128)S(1)} %get-tuple-element.4.offs_smem.offs_ref, f32[128,128]{1,0:T(8,128)S(1)} %bitcast.12), custom_call_target="tpu_custom_call" | custom-call | tf_op jit(solution)/shard_map/finish/pallas_call | solution.py:286
  (1 shorter events, 0.0 us)
Async XLA Ops:
  32.0 6.3 %collective-permute-start = (f32[32,128]{1,0:T(8,128)S(1)}, f32[32,128]{1,0:T(8,128)S(1)}, u32[]{:S(2)}, u32[]{:S(2)}) collective-permute-start(f32[32,128]{1,0:T(8,128)S(1)} %edge_looks.1), channel_id=1, source_target_pairs={{17,16},{16,17},{49,48},{48,49},{81,80},{80,81},{113,112},{112,113... | collective-permute-start | bytes 49160 | tf_op jit(solution)/shard_map/ppermute | solution.py:317

commit v4 on v3

--- a/solution.py
+++ b/solution.py
@@ -75,36 +75,44 @@
     )(tiles, offsets.T)
 
 
-def edge_kernel(offs_ref, tiles_ref, edge_ref, shifted, stack):
+def edge_kernel(offs_ref, tiles_ref, edge_ref, tiles, shifted, stack):
     half = own_half()
     lanes = lax.broadcasted_iota(jnp.int32, (DATES, 128), 1)
     packed = []
     for p in range(2):
+        for d in range(DATES):
+            tile = tiles_ref[pl.ds(pl.multiple_of(32 * d + 16 * p + 8 * half, 8), 8), :]
+            tiles[p, 8 * d : 8 * d + 8, :] = tile
         value = jnp.zeros((DATES, 128), jnp.float32)
         for i in range(8):
-            row = tiles_ref[pl.ds(16 * p + 8 * half + i, DATES, stride=32), :]
+            row = tiles[p, pl.ds(i, DATES, stride=8), :]
             value = jnp.where(lanes // 16 == i, pltpu.roll(row, 16 * (half + i), 1), value)
         packed.append(value)
-    packed.append(packed[0] * packed[0] + packed[1] * packed[1])
-    for q in range(3):
-        shifted[q, 0:DATES, :] = packed[q]
-        shifted[q, DATES : DATES + 8, :] = jnp.zeros((8, 128), jnp.float32)
+    for p in range(2):
+        shifted[p, 0:DATES, :] = packed[p]
+        shifted[p, DATES : DATES + 8, :] = jnp.zeros((8, 128), jnp.float32)
     offs = offs_ref[...]
-    looks = [None] * (MAPS - 1) + [packed[2]]
-    for j in range(SLOTS):
-        offset = jnp.broadcast_to(offs[:, j : j + 1], (DATES, 128))
-        partner = [jnp.zeros((DATES, 128), jnp.float32)] * 3
+    for top in range(0, DATES, 16):
+        rows = slice(top, top + 16)
+        real, imag = packed[0][rows, :], packed[1][rows, :]
+        offset = [jnp.broadcast_to(offs[rows, j : j + 1], (16, 128)) for j in range(SLOTS)]
+        partner = [[jnp.zeros((16, 128), jnp.float32)] * 2 for j in range(SLOTS)]
         for step in range(1, MAX_OFFSET + 1):
-            partner = [jnp.where(offset == step, shifted[q, step : step + DATES, :], partner[q]) for q in range(3)]
-        looks[j] = packed[0] * partner[0] + packed[1] * partner[1]
-        looks[SLOTS + j] = packed[1] * partner[0] - packed[0] * partner[1]
-        looks[2 * SLOTS + j] = partner[2]
-    for m in range(MAPS):
-        for q, part in enumerate(two_parts(looks[m] / 64.0)):
-            stack[DATES * m : DATES * m + DATES, 128 * q : 128 * q + 128] = part
-    lane = lax.broadcasted_iota(jnp.int32, (256, 128), 0)
-    place = lax.broadcasted_iota(jnp.int32, (256, 128), 1)
-    sums = ((lane % 128) // 64 == place % 2).astype(jnp.bfloat16)
+            later = [shifted[p, top + step : top + step + 16, :] for p in range(2)]
+            for j in range(SLOTS):
+                here = offset[j] == step
+                partner[j] = [jnp.where(here, later[p], partner[j][p]) for p in range(2)]
+        looks = [real * b[0] + imag * b[1] for b in partner]
+        looks += [imag * b[0] - real * b[1] for b in partner]
+        looks += [b[0] * b[0] + b[1] * b[1] for b in partner]
+        looks += [real * real + imag * imag]
+        for m in range(MAPS):
+            for q, part in enumerate(two_parts(looks[m] / 64.0)):
+                stack[DATES * m + top : DATES * m + top + 16, 128 * q : 128 * q + 128] = part
+    lane = lax.broadcasted_iota(jnp.int32, (128, 128), 0)
+    place = lax.broadcasted_iota(jnp.int32, (128, 128), 1)
+    sums = (lane // 64 == place % 2).astype(jnp.bfloat16)
+    sums = jnp.concatenate([sums, sums], axis=0)
     out = jnp.dot(stack[...], sums, preferred_element_type=jnp.float32)
     edge = jnp.zeros((DATES, 128), jnp.float32)
     for m in range(MAPS):
@@ -119,7 +127,8 @@
         in_specs=[VMEM, VMEM],
         out_specs=VMEM,
         scratch_shapes=[
-            pltpu.VMEM((3, DATES + 8, 128), jnp.float32),
+            pltpu.VMEM((2, 8 * DATES, 128), jnp.float32),
+            pltpu.VMEM((2, DATES + 8, 128), jnp.float32),
             pltpu.VMEM((MAPS * DATES, 256), jnp.bfloat16),
         ],
         name="edge_looks",
@@ -235,16 +244,15 @@
         for half in range(2)
     ]
 
+    second = [pltpu.roll(block, 16, 1) for block in blocks[1]]
+    halos = jnp.where(lanes < HALO_LANE + 32, blocks[0][3], pltpu.roll(blocks[1][3], 33, 1))
+
     def cells(m, r):
         g = 2 * m + r
         k, at = g // 8, 16 * (g % 8)
-        value = jnp.zeros((16, 128), jnp.float32)
-        for half in range(2):
-            piece = pltpu.roll(blocks[half][k], (16 * half - at) % 128, 1)
-            value = jnp.where(lanes // 16 == half, piece, value)
-        left = pltpu.roll(blocks[0][3], (127 - HALO_LANE - g) % 128, 1)
-        right = pltpu.roll(blocks[1][3], (32 - HALO_LANE - g) % 128, 1)
-        return jnp.where(lanes == 127, left, jnp.where(lanes == 32, right, value))
+        both = jnp.where(lanes // 16 == g % 8, blocks[0][k], second[k])
+        halo = pltpu.roll(halos, (127 - HALO_LANE - g) % 128, 1)
+        return jnp.where(lanes < 32, pltpu.roll(both, (128 - at) % 128, 1), halo)
 
     row = lax.broadcasted_iota(jnp.int32, (16, 128), 0)
 

time: 55.7 us -> 54.8 us (0.984)
  Pallas kernels: 5.72 us -> 4.86 us
    pallas_call x1, Pallas kernels: 1.86 us -> 1.12 us  [finish(): pl.pallas_call(finish_kernel, out_shape=(jax.ShapeDtypeStruct((2, 1, SLOT...]
where the time goes in v4:
time: 54.8 us; the launch traced here: 54.6 us
  blocking collectives  45 us (82%)
  Pallas kernels  4.86 us (9%)
  waiting for transfers between devices  2.12 us (4%)
  starting transfers between devices  1.92 us (4%)
  between operations  0.66 us (1%)
    all_to_all x1, blocking collectives, shards(): lax.all_to_all(tiles.reshape(DATES, 32, 128), 'date', 0, 0, tiled=True)  29.7 us
    all_to_all x1, blocking collectives, shards(): lax.all_to_all(looks.reshape(DATES, 4, 128), 'date', 0, 0, tiled=True)  15.3 us
    pallas_call x1, Pallas kernels, local_looks(): pl.pallas_call(looks_kernel, out_shape=pltpu.VMEM((4 * DATES, 128), jnp.f...  2.21 us
    ppermute x1, waiting for transfers between devices, shards(): lax.ppermute(edge, ('date', 'col'), edge_pairs(DATES, lax.axis_size('col')))  2.12 us
    ppermute x1, starting transfers between devices, shards(): lax.ppermute(edge, ('date', 'col'), edge_pairs(DATES, lax.axis_size('col')))  1.92 us
    pallas_call x1, Pallas kernels, pieces(): pl.pallas_call(pieces_kernel, out_shape=(pltpu.VMEM((16, 2, 2, 2, 8, 128)...  1.15 us
    pallas_call x1, Pallas kernels, finish(): pl.pallas_call(finish_kernel, out_shape=(jax.ShapeDtypeStruct((2, 1, SLOT...  1.12 us
  transfers between devices with their start and end apart: 1, of which 1 were waited for; matrix products, arithmetic and copies ran while one was open for 0% of the time, Pallas kernels for 4%

profile of v4, /device:TPU:32, one launch (start us, length us, event | category | flops | bytes accessed | tf_op | source)
XLA Modules:
  0.0 54.6 jit_solution(11030501660720607766)
XLA Ops:
  0.6 1.2 %pieces.1 = (f32[16,2,2,2,8,128]{5,4,3,2,1,0:T(8,128)S(1)}, s32[32,4]{1,0:T(8,128)S(1)}) custom-call(f32[2,16,2,2,8,128]{5,4,3,2,1,0:T(8,128)} %bitcast.13, s32[4,32]{1,0:T(4,128)} %bitcast.14), custom_call_target="tpu_custom_call" | custom-call | tf_op jit(solution)/shard_map/pieces/pallas_call | solution.py:61
  1.8 29.7 %all_to_all.10 = f32[32,32,128]{2,1,0:T(8,128)S(1)} all-to-all(f32[32,32,128]{2,1,0:T(8,128)S(1)} %bitcast.11), channel_id=1, replica_groups=mesh['date'=32,'col'=16] {'date'}, dimensions={0} | all-to-all | bytes 1048576 | tf_op jit(solution)/shard_map/all_to_all | solution.py:322
  31.5 0.4 edge_looks.1
  31.8 1.9 %collective-permute-start = (f32[32,128]{1,0:T(8,128)S(1)}, f32[32,128]{1,0:T(8,128)S(1)}, u32[]{:S(2)}, u32[]{:S(2)}) collective-permute-start(f32[32,128]{1,0:T(8,128)S(1)} %edge_looks.1), channel_id=1, source_target_pairs={{17,16},{16,17},{49,48},{48,49},{81,80},{80,81},{113,112},{112,113... | collective-permute-start | bytes 49160 | tf_op jit(solution)/shard_map/ppermute | solution.py:325
  33.8 2.2 %looks.1.looks_ref = f32[128,128]{1,0:T(8,128)S(1)} custom-call(s32[32,4]{1,0:T(8,128)S(1)} %get-tuple-element.4.offs_smem.offs_ref, s32[32,4]{1,0:T(8,128)S(1)} %get-tuple-element.4.offs_smem.offs_ref, f32[1024,128]{1,0:T(8,128)S(1)} %bitcast.9), custom_call_target="tpu_custom_call" | custom-call | tf_op jit(solution)/shard_map/looks/pallas_call | solution.py:210
  36.0 2.1 %collective-permute-done.edge_ref = f32[32,128]{1,0:T(8,128)S(1)} collective-permute-done((f32[32,128]{1,0:T(8,128)S(1)}, f32[32,128]{1,0:T(8,128)S(1)}, u32[]{:S(2)}, u32[]{:S(2)}) %collective-permute-start) | collective-permute-done | bytes 16416 | tf_op jit(solution)/shard_map/ppermute | solution.py:325
  38.1 15.3 %all_to_all.11 = f32[32,4,128]{2,1,0:T(4,128)S(1)} all-to-all(f32[32,4,128]{2,1,0:T(4,128)S(1)} %bitcast.10), channel_id=1, replica_groups=mesh['date'=32,'col'=16] {'date'}, dimensions={0} | all-to-all | bytes 131072 | tf_op jit(solution)/shard_map/all_to_all | solution.py:327
  53.5 1.1 %finish.1 = (f32[2,1,4,32,32]{4,3,2,1,0:T(8,128)}, f32[1,4,32,32]{3,2,1,0:T(8,128)}) custom-call(s32[32,4]{1,0:T(8,128)S(1)} %get-tuple-element.4.offs_smem.offs_ref, f32[128,128]{1,0:T(8,128)S(1)} %bitcast.12), custom_call_target="tpu_custom_call" | custom-call | tf_op jit(solution)/shard_map/finish/pallas_call | solution.py:294
  (1 shorter events, 0.0 us)
Async XLA Ops:
  31.8 6.3 %collective-permute-start = (f32[32,128]{1,0:T(8,128)S(1)}, f32[32,128]{1,0:T(8,128)S(1)}, u32[]{:S(2)}, u32[]{:S(2)}) collective-permute-start(f32[32,128]{1,0:T(8,128)S(1)} %edge_looks.1), channel_id=1, source_target_pairs={{17,16},{16,17},{49,48},{48,49},{81,80},{80,81},{113,112},{112,113... | collective-permute-start | bytes 49160 | tf_op jit(solution)/shard_map/ppermute | solution.py:325

commit v5 on v4

--- a/solution.py
+++ b/solution.py
@@ -35,25 +35,20 @@
     return high, (value - high.astype(jnp.float32)).astype(jnp.bfloat16)
 
 
-def pieces_kernel(slc_ref, slots_ref, out_ref, offs_ref, slots, sems, slots_sem):
+def pieces_kernel(slc_ref, slots_ref, out_ref, offs_ref, planes, slots, sems, slots_sem):
     odd = odd_col()
     first = pltpu.make_async_copy(slots_ref, slots, slots_sem)
     first.start()
-    copies = [
-        pltpu.make_async_copy(
-            slc_ref.at[p, :, half],
-            out_ref.at[:, jnp.bitwise_xor(odd, half), p],
-            sems.at[p, half],
-        )
-        for p in range(2)
-        for half in range(2)
-    ]
+    copies = [pltpu.make_async_copy(slc_ref.at[p], planes.at[p], sems.at[p]) for p in range(2)]
     for copy in copies:
         copy.start()
     first.wait()
     offs_ref[...] = slots[...].T
-    for copy in copies:
+    for p, copy in enumerate(copies):
         copy.wait()
+        for block in range(16):
+            for half in range(2):
+                out_ref[block, jnp.bitwise_xor(odd, half), p] = planes[p, block, half]
 
 
 def pieces(slc, offsets):
@@ -67,8 +62,9 @@
         in_specs=[ANY, ANY],
         out_specs=(VMEM, VMEM),
         scratch_shapes=[
+            pltpu.VMEM((2, 16, 2, 2, 8, 128), jnp.float32),
             pltpu.VMEM((SLOTS, DATES), jnp.int32),
-            pltpu.SemaphoreType.DMA((2, 2)),
+            pltpu.SemaphoreType.DMA((2,)),
             pltpu.SemaphoreType.DMA,
         ],
         name="pieces",
@@ -107,23 +103,26 @@
         looks += [b[0] * b[0] + b[1] * b[1] for b in partner]
         looks += [real * real + imag * imag]
         for m in range(MAPS):
-            for q, part in enumerate(two_parts(looks[m] / 64.0)):
+            for q, part in enumerate(two_parts(looks[m])):
                 stack[DATES * m + top : DATES * m + top + 16, 128 * q : 128 * q + 128] = part
     lane = lax.broadcasted_iota(jnp.int32, (128, 128), 0)
     place = lax.broadcasted_iota(jnp.int32, (128, 128), 1)
-    sums = (lane // 64 == place % 2).astype(jnp.bfloat16)
+    sums = jnp.where(lane // 64 == place % 2, 1.0 / 64.0, 0.0).astype(jnp.bfloat16)
     sums = jnp.concatenate([sums, sums], axis=0)
     out = jnp.dot(stack[...], sums, preferred_element_type=jnp.float32)
-    edge = jnp.zeros((DATES, 128), jnp.float32)
-    for m in range(MAPS):
-        edge = jnp.where((lanes - HALO_LANE) // 2 == m, out[DATES * m : DATES * m + DATES, :], edge)
-    edge_ref[...] = jnp.where(lanes >= HALO_LANE, edge, 0.0)
+    lanes = lax.broadcasted_iota(jnp.int32, (8, 128), 1)
+    block = jnp.zeros((8, 128), jnp.float32)
+    for x in range(4):
+        for m in range(MAPS):
+            at = DATES * m + 8 * x
+            block = jnp.where(lanes // 2 == 16 * x + m, out[at : at + 8, :], block)
+    edge_ref[...] = block
 
 
 def edge_looks(offsets, tiles):
     return pl.pallas_call(
         edge_kernel,
-        out_shape=pltpu.VMEM((DATES, 128), jnp.float32),
+        out_shape=pltpu.VMEM((8, 128), jnp.float32),
         in_specs=[VMEM, VMEM],
         out_specs=VMEM,
         scratch_shapes=[
@@ -221,8 +220,12 @@
 
 
 def with_edge_kernel(looks_ref, edge_ref, out_ref):
-    rows = pl.ds(3, DATES, stride=4)
-    out_ref[rows, :] = looks_ref[rows, :] + edge_ref[...]
+    edge = edge_ref[...]
+    lanes = lax.broadcasted_iota(jnp.int32, (8, 128), 1)
+    for x in range(4):
+        rows = pl.ds(DATES * x + 3, 8, stride=4)
+        piece = pltpu.roll(edge, (HALO_LANE - 32 * x) % 128, 1)
+        out_ref[rows, :] = jnp.where(lanes // 32 == HALO_LANE // 32, piece, looks_ref[rows, :])
 
 
 def with_edge(looks, edge):

time: 54.8 us -> 54.7 us (level)
  no operation moved by 1% of the time
where the time goes in v5:
time: 54.7 us; the launch traced here: 54.5 us
  blocking collectives  45 us (82%)
  Pallas kernels  4.89 us (9%)
  waiting for transfers between devices  2 us (4%)
  starting transfers between devices  1.92 us (4%)
  between operations  0.66 us (1%)
    all_to_all x1, blocking collectives, shards(): lax.all_to_all(tiles.reshape(DATES, 32, 128), 'date', 0, 0, tiled=True)  29.7 us
    all_to_all x1, blocking collectives, shards(): lax.all_to_all(looks.reshape(DATES, 4, 128), 'date', 0, 0, tiled=True)  15.3 us
    pallas_call x1, Pallas kernels, local_looks(): pl.pallas_call(looks_kernel, out_shape=pltpu.VMEM((4 * DATES, 128), jnp.f...  2.21 us
    ppermute x1, waiting for transfers between devices, shards(): lax.ppermute(edge, ('date', 'col'), edge_pairs(DATES, lax.axis_size('col')))  2 us
    ppermute x1, starting transfers between devices, shards(): lax.ppermute(edge, ('date', 'col'), edge_pairs(DATES, lax.axis_size('col')))  1.92 us
    pallas_call x1, Pallas kernels, finish(): pl.pallas_call(finish_kernel, out_shape=(jax.ShapeDtypeStruct((2, 1, SLOT...  1.12 us
  transfers between devices with their start and end apart: 1, of which 1 were waited for; matrix products, arithmetic and copies ran while one was open for 0% of the time, Pallas kernels for 4%

profile of v5, /device:TPU:32, one launch (start us, length us, event | category | flops | bytes accessed | tf_op | source)
XLA Modules:
  0.0 54.5 jit_solution(4697118214106395949)
XLA Ops:
  0.6 1.1 %pieces.1 = (f32[16,2,2,2,8,128]{5,4,3,2,1,0:T(8,128)S(1)}, s32[32,4]{1,0:T(8,128)S(1)}) custom-call(f32[2,16,2,2,8,128]{5,4,3,2,1,0:T(8,128)} %bitcast.13, s32[4,32]{1,0:T(4,128)} %bitcast.14), custom_call_target="tpu_custom_call" | custom-call | tf_op jit(solution)/shard_map/pieces/pallas_call | solution.py:56
  1.7 29.7 %all_to_all.10 = f32[32,32,128]{2,1,0:T(8,128)S(1)} all-to-all(f32[32,32,128]{2,1,0:T(8,128)S(1)} %bitcast.11), channel_id=1, replica_groups=mesh['date'=32,'col'=16] {'date'}, dimensions={0} | all-to-all | bytes 1048576 | tf_op jit(solution)/shard_map/all_to_all | solution.py:325
  31.4 0.4 edge_looks.1
  31.8 1.9 %collective-permute-start = (f32[8,128]{1,0:T(8,128)S(1)}, f32[8,128]{1,0:T(8,128)S(1)}, u32[]{:S(2)}, u32[]{:S(2)}) collective-permute-start(f32[8,128]{1,0:T(8,128)S(1)} %edge_looks.1), channel_id=1, source_target_pairs={{17,16},{16,17},{49,48},{48,49},{81,80},{80,81},{113,112},{112,113... | collective-permute-start | bytes 12296 | tf_op jit(solution)/shard_map/ppermute | solution.py:328
  33.7 2.2 %looks.1.looks_ref = f32[128,128]{1,0:T(8,128)S(1)} custom-call(s32[32,4]{1,0:T(8,128)S(1)} %get-tuple-element.4.offs_smem.offs_ref, s32[32,4]{1,0:T(8,128)S(1)} %get-tuple-element.4.offs_smem.offs_ref, f32[1024,128]{1,0:T(8,128)S(1)} %bitcast.9), custom_call_target="tpu_custom_call" | custom-call | tf_op jit(solution)/shard_map/looks/pallas_call | solution.py:209
  35.9 2.0 %collective-permute-done.edge_ref = f32[8,128]{1,0:T(8,128)S(1)} collective-permute-done((f32[8,128]{1,0:T(8,128)S(1)}, f32[8,128]{1,0:T(8,128)S(1)}, u32[]{:S(2)}, u32[]{:S(2)}) %collective-permute-start) | collective-permute-done | bytes 4128 | tf_op jit(solution)/shard_map/ppermute | solution.py:328
  37.9 0.1 with_edge.1
  38.0 15.3 %all_to_all.11 = f32[32,4,128]{2,1,0:T(4,128)S(1)} all-to-all(f32[32,4,128]{2,1,0:T(4,128)S(1)} %bitcast.10), channel_id=1, replica_groups=mesh['date'=32,'col'=16] {'date'}, dimensions={0} | all-to-all | bytes 131072 | tf_op jit(solution)/shard_map/all_to_all | solution.py:330
  53.4 1.1 %finish.1 = (f32[2,1,4,32,32]{4,3,2,1,0:T(8,128)}, f32[1,4,32,32]{3,2,1,0:T(8,128)}) custom-call(s32[32,4]{1,0:T(8,128)S(1)} %get-tuple-element.4.offs_smem.offs_ref, f32[128,128]{1,0:T(8,128)S(1)} %bitcast.12), custom_call_target="tpu_custom_call" | custom-call | tf_op jit(solution)/shard_map/finish/pallas_call | solution.py:297
Async XLA Ops:
  31.8 6.1 %collective-permute-start = (f32[8,128]{1,0:T(8,128)S(1)}, f32[8,128]{1,0:T(8,128)S(1)}, u32[]{:S(2)}, u32[]{:S(2)}) collective-permute-start(f32[8,128]{1,0:T(8,128)S(1)} %edge_looks.1), channel_id=1, source_target_pairs={{17,16},{16,17},{49,48},{48,49},{81,80},{80,81},{113,112},{112,113... | collective-permute-start | bytes 12296 | tf_op jit(solution)/shard_map/ppermute | solution.py:328

commit v6 on v5

--- a/solution.py
+++ b/solution.py
@@ -110,19 +110,16 @@
     sums = jnp.where(lane // 64 == place % 2, 1.0 / 64.0, 0.0).astype(jnp.bfloat16)
     sums = jnp.concatenate([sums, sums], axis=0)
     out = jnp.dot(stack[...], sums, preferred_element_type=jnp.float32)
-    lanes = lax.broadcasted_iota(jnp.int32, (8, 128), 1)
-    block = jnp.zeros((8, 128), jnp.float32)
-    for x in range(4):
-        for m in range(MAPS):
-            at = DATES * m + 8 * x
-            block = jnp.where(lanes // 2 == 16 * x + m, out[at : at + 8, :], block)
-    edge_ref[...] = block
+    edge = jnp.zeros((DATES, 128), jnp.float32)
+    for m in range(MAPS):
+        edge = jnp.where((lanes - HALO_LANE) // 2 == m, out[DATES * m : DATES * m + DATES, :], edge)
+    edge_ref[...] = jnp.where(lanes >= HALO_LANE, edge, 0.0)
 
 
 def edge_looks(offsets, tiles):
     return pl.pallas_call(
         edge_kernel,
-        out_shape=pltpu.VMEM((8, 128), jnp.float32),
+        out_shape=pltpu.VMEM((DATES, 128), jnp.float32),
         in_specs=[VMEM, VMEM],
         out_specs=VMEM,
         scratch_shapes=[
@@ -220,12 +217,8 @@
 
 
 def with_edge_kernel(looks_ref, edge_ref, out_ref):
-    edge = edge_ref[...]
-    lanes = lax.broadcasted_iota(jnp.int32, (8, 128), 1)
-    for x in range(4):
-        rows = pl.ds(DATES * x + 3, 8, stride=4)
-        piece = pltpu.roll(edge, (HALO_LANE - 32 * x) % 128, 1)
-        out_ref[rows, :] = jnp.where(lanes // 32 == HALO_LANE // 32, piece, looks_ref[rows, :])
+    rows = pl.ds(3, DATES, stride=4)
+    out_ref[rows, :] = looks_ref[rows, :] + edge_ref[...]
 
 
 def with_edge(looks, edge):

time: 54.7 us -> 54.7 us (level)
  no operation moved by 1% of the time
where the time goes in v6:
time: 54.7 us; the launch traced here: 54.5 us
  blocking collectives  45 us (82%)
  Pallas kernels  4.8 us (9%)
  waiting for transfers between devices  2.12 us (4%)
  starting transfers between devices  1.92 us (4%)
  between operations  0.66 us (1%)
    all_to_all x1, blocking collectives, shards(): lax.all_to_all(tiles.reshape(DATES, 32, 128), 'date', 0, 0, tiled=True)  29.7 us
    all_to_all x1, blocking collectives, shards(): lax.all_to_all(looks.reshape(DATES, 4, 128), 'date', 0, 0, tiled=True)  15.3 us
    pallas_call x1, Pallas kernels, local_looks(): pl.pallas_call(looks_kernel, out_shape=pltpu.VMEM((4 * DATES, 128), jnp.f...  2.21 us
    ppermute x1, waiting for transfers between devices, shards(): lax.ppermute(edge, ('date', 'col'), edge_pairs(DATES, lax.axis_size('col')))  2.12 us
    ppermute x1, starting transfers between devices, shards(): lax.ppermute(edge, ('date', 'col'), edge_pairs(DATES, lax.axis_size('col')))  1.92 us
    pallas_call x1, Pallas kernels, finish(): pl.pallas_call(finish_kernel, out_shape=(jax.ShapeDtypeStruct((2, 1, SLOT...  1.12 us
  transfers between devices with their start and end apart: 1, of which 1 were waited for; matrix products, arithmetic and copies ran while one was open for 0% of the time, Pallas kernels for 4%

profile of v6, /device:TPU:32, one launch (start us, length us, event | category | flops | bytes accessed | tf_op | source)
XLA Modules:
  0.0 54.5 jit_solution(18427914484717305703)
XLA Ops:
  0.6 1.1 %pieces.1 = (f32[16,2,2,2,8,128]{5,4,3,2,1,0:T(8,128)S(1)}, s32[32,4]{1,0:T(8,128)S(1)}) custom-call(f32[2,16,2,2,8,128]{5,4,3,2,1,0:T(8,128)} %bitcast.13, s32[4,32]{1,0:T(4,128)} %bitcast.14), custom_call_target="tpu_custom_call" | custom-call | tf_op jit(solution)/shard_map/pieces/pallas_call | solution.py:56
  1.7 29.7 %all_to_all.10 = f32[32,32,128]{2,1,0:T(8,128)S(1)} all-to-all(f32[32,32,128]{2,1,0:T(8,128)S(1)} %bitcast.11), channel_id=1, replica_groups=mesh['date'=32,'col'=16] {'date'}, dimensions={0} | all-to-all | bytes 1048576 | tf_op jit(solution)/shard_map/all_to_all | solution.py:318
  31.4 0.4 edge_looks.1
  31.8 1.9 %collective-permute-start = (f32[32,128]{1,0:T(8,128)S(1)}, f32[32,128]{1,0:T(8,128)S(1)}, u32[]{:S(2)}, u32[]{:S(2)}) collective-permute-start(f32[32,128]{1,0:T(8,128)S(1)} %edge_looks.1), channel_id=1, source_target_pairs={{17,16},{16,17},{49,48},{48,49},{81,80},{80,81},{113,112},{112,113... | collective-permute-start | bytes 49160 | tf_op jit(solution)/shard_map/ppermute | solution.py:321
  33.7 2.2 %looks.1.looks_ref = f32[128,128]{1,0:T(8,128)S(1)} custom-call(s32[32,4]{1,0:T(8,128)S(1)} %get-tuple-element.4.offs_smem.offs_ref, s32[32,4]{1,0:T(8,128)S(1)} %get-tuple-element.4.offs_smem.offs_ref, f32[1024,128]{1,0:T(8,128)S(1)} %bitcast.9), custom_call_target="tpu_custom_call" | custom-call | tf_op jit(solution)/shard_map/looks/pallas_call | solution.py:206
  35.9 2.1 %collective-permute-done.edge_ref = f32[32,128]{1,0:T(8,128)S(1)} collective-permute-done((f32[32,128]{1,0:T(8,128)S(1)}, f32[32,128]{1,0:T(8,128)S(1)}, u32[]{:S(2)}, u32[]{:S(2)}) %collective-permute-start) | collective-permute-done | bytes 16416 | tf_op jit(solution)/shard_map/ppermute | solution.py:321
  38.1 15.3 %all_to_all.11 = f32[32,4,128]{2,1,0:T(4,128)S(1)} all-to-all(f32[32,4,128]{2,1,0:T(4,128)S(1)} %bitcast.10), channel_id=1, replica_groups=mesh['date'=32,'col'=16] {'date'}, dimensions={0} | all-to-all | bytes 131072 | tf_op jit(solution)/shard_map/all_to_all | solution.py:323
  53.4 1.1 %finish.1 = (f32[2,1,4,32,32]{4,3,2,1,0:T(8,128)}, f32[1,4,32,32]{3,2,1,0:T(8,128)}) custom-call(s32[32,4]{1,0:T(8,128)S(1)} %get-tuple-element.4.offs_smem.offs_ref, f32[128,128]{1,0:T(8,128)S(1)} %bitcast.12), custom_call_target="tpu_custom_call" | custom-call | tf_op jit(solution)/shard_map/finish/pallas_call | solution.py:290
  (1 shorter events, 0.0 us)
Async XLA Ops:
  31.8 6.3 %collective-permute-start = (f32[32,128]{1,0:T(8,128)S(1)}, f32[32,128]{1,0:T(8,128)S(1)}, u32[]{:S(2)}, u32[]{:S(2)}) collective-permute-start(f32[32,128]{1,0:T(8,128)S(1)} %edge_looks.1), channel_id=1, source_target_pairs={{17,16},{16,17},{49,48},{48,49},{81,80},{80,81},{113,112},{112,113... | collective-permute-start | bytes 49160 | tf_op jit(solution)/shard_map/ppermute | solution.py:321

commit v7 on v6

--- a/solution.py
+++ b/solution.py
@@ -270,16 +270,15 @@
     for j in range(SLOTS):
         live = jnp.broadcast_to(lives[:, j : j + 1], (16, 128))
         real, imag = window(j), window(SLOTS + j)
-        for p in range(2):
-            copy = pltpu.make_async_copy(inter_ref.at[p, 0, j], inter_out.at[p, 0, j], sems.at[p, j])
-            copy.start()
-            copies.append(copy)
+        both = pltpu.make_async_copy(inter_ref.at[:, 0, j], inter_out.at[:, 0, j], sems.at[0, j])
+        both.start()
+        copies.append(both)
         partner = window(2 * SLOTS + j)
         for r in range(2):
             magnitude = jnp.sqrt(real[r] * real[r] + imag[r] * imag[r])
             value = magnitude / (jnp.sqrt((own[r] * live) * partner[r]) + epsilon)
             coh_ref[0, j, pl.ds(r, 16, stride=2), :] = value[:, :32]
-        last = pltpu.make_async_copy(coh_ref.at[0, j], coh_out.at[0, j], sems.at[2, j])
+        last = pltpu.make_async_copy(coh_ref.at[0, j], coh_out.at[0, j], sems.at[1, j])
         last.start()
         copies.append(last)
     for copy in copies:
@@ -298,7 +297,7 @@
         scratch_shapes=[
             pltpu.VMEM((2, 1, SLOTS, 32, 32), jnp.float32),
             pltpu.VMEM((1, SLOTS, 32, 32), jnp.float32),
-            pltpu.SemaphoreType.DMA((3, SLOTS)),
+            pltpu.SemaphoreType.DMA((2, SLOTS)),
         ],
         name="finish",
     )(in_vmem(offsets), in_vmem(looks))

time: 54.7 us -> 54.7 us (level)
  no operation moved by 1% of the time
where the time goes in v7:
time: 54.7 us; the launch traced here: 54.5 us
  blocking collectives  45 us (82%)
  Pallas kernels  4.77 us (9%)
  waiting for transfers between devices  2.12 us (4%)
  starting transfers between devices  1.92 us (4%)
  between operations  0.66 us (1%)
    all_to_all x1, blocking collectives, shards(): lax.all_to_all(tiles.reshape(DATES, 32, 128), 'date', 0, 0, tiled=True)  29.7 us
    all_to_all x1, blocking collectives, shards(): lax.all_to_all(looks.reshape(DATES, 4, 128), 'date', 0, 0, tiled=True)  15.3 us
    pallas_call x1, Pallas kernels, local_looks(): pl.pallas_call(looks_kernel, out_shape=pltpu.VMEM((4 * DATES, 128), jnp.f...  2.21 us
    ppermute x1, waiting for transfers between devices, shards(): lax.ppermute(edge, ('date', 'col'), edge_pairs(DATES, lax.axis_size('col')))  2.12 us
    ppermute x1, starting transfers between devices, shards(): lax.ppermute(edge, ('date', 'col'), edge_pairs(DATES, lax.axis_size('col')))  1.92 us
  transfers between devices with their start and end apart: 1, of which 1 were waited for; matrix products, arithmetic and copies ran while one was open for 0% of the time, Pallas kernels for 4%

profile of v7, /device:TPU:32, one launch (start us, length us, event | category | flops | bytes accessed | tf_op | source)
XLA Modules:
  0.0 54.5 jit_solution(8391636154281192423)
XLA Ops:
  0.6 1.1 %pieces.1 = (f32[16,2,2,2,8,128]{5,4,3,2,1,0:T(8,128)S(1)}, s32[32,4]{1,0:T(8,128)S(1)}) custom-call(f32[2,16,2,2,8,128]{5,4,3,2,1,0:T(8,128)} %bitcast.13, s32[4,32]{1,0:T(4,128)} %bitcast.14), custom_call_target="tpu_custom_call" | custom-call | tf_op jit(solution)/shard_map/pieces/pallas_call | solution.py:56
  1.7 29.7 %all_to_all.10 = f32[32,32,128]{2,1,0:T(8,128)S(1)} all-to-all(f32[32,32,128]{2,1,0:T(8,128)S(1)} %bitcast.11), channel_id=1, replica_groups=mesh['date'=32,'col'=16] {'date'}, dimensions={0} | all-to-all | bytes 1048576 | tf_op jit(solution)/shard_map/all_to_all | solution.py:317
  31.4 0.4 edge_looks.1
  31.8 1.9 %collective-permute-start = (f32[32,128]{1,0:T(8,128)S(1)}, f32[32,128]{1,0:T(8,128)S(1)}, u32[]{:S(2)}, u32[]{:S(2)}) collective-permute-start(f32[32,128]{1,0:T(8,128)S(1)} %edge_looks.1), channel_id=1, source_target_pairs={{17,16},{16,17},{49,48},{48,49},{81,80},{80,81},{113,112},{112,113... | collective-permute-start | bytes 49160 | tf_op jit(solution)/shard_map/ppermute | solution.py:320
  33.7 2.2 %looks.1.looks_ref = f32[128,128]{1,0:T(8,128)S(1)} custom-call(s32[32,4]{1,0:T(8,128)S(1)} %get-tuple-element.4.offs_smem.offs_ref, s32[32,4]{1,0:T(8,128)S(1)} %get-tuple-element.4.offs_smem.offs_ref, f32[1024,128]{1,0:T(8,128)S(1)} %bitcast.9), custom_call_target="tpu_custom_call" | custom-call | tf_op jit(solution)/shard_map/looks/pallas_call | solution.py:206
  35.9 2.1 %collective-permute-done.edge_ref = f32[32,128]{1,0:T(8,128)S(1)} collective-permute-done((f32[32,128]{1,0:T(8,128)S(1)}, f32[32,128]{1,0:T(8,128)S(1)}, u32[]{:S(2)}, u32[]{:S(2)}) %collective-permute-start) | collective-permute-done | bytes 16416 | tf_op jit(solution)/shard_map/ppermute | solution.py:320
  38.1 15.3 %all_to_all.11 = f32[32,4,128]{2,1,0:T(4,128)S(1)} all-to-all(f32[32,4,128]{2,1,0:T(4,128)S(1)} %bitcast.10), channel_id=1, replica_groups=mesh['date'=32,'col'=16] {'date'}, dimensions={0} | all-to-all | bytes 131072 | tf_op jit(solution)/shard_map/all_to_all | solution.py:322
  53.4 1.1 %finish.1 = (f32[2,1,4,32,32]{4,3,2,1,0:T(8,128)}, f32[1,4,32,32]{3,2,1,0:T(8,128)}) custom-call(s32[32,4]{1,0:T(8,128)S(1)} %get-tuple-element.4.offs_smem.offs_ref, f32[128,128]{1,0:T(8,128)S(1)} %bitcast.12), custom_call_target="tpu_custom_call" | custom-call | tf_op jit(solution)/shard_map/finish/pallas_call | solution.py:289
  (1 shorter events, 0.0 us)
Async XLA Ops:
  31.8 6.3 %collective-permute-start = (f32[32,128]{1,0:T(8,128)S(1)}, f32[32,128]{1,0:T(8,128)S(1)}, u32[]{:S(2)}, u32[]{:S(2)}) collective-permute-start(f32[32,128]{1,0:T(8,128)S(1)} %edge_looks.1), channel_id=1, source_target_pairs={{17,16},{16,17},{49,48},{48,49},{81,80},{80,81},{113,112},{112,113... | collective-permute-start | bytes 49160 | tf_op jit(solution)/shard_map/ppermute | solution.py:320

commit v8 on v7

--- a/solution.py
+++ b/solution.py
@@ -38,10 +38,10 @@
 def pieces_kernel(slc_ref, slots_ref, out_ref, offs_ref, planes, slots, sems, slots_sem):
     odd = odd_col()
     first = pltpu.make_async_copy(slots_ref, slots, slots_sem)
-    first.start()
     copies = [pltpu.make_async_copy(slc_ref.at[p], planes.at[p], sems.at[p]) for p in range(2)]
     for copy in copies:
         copy.start()
+    first.start()
     first.wait()
     offs_ref[...] = slots[...].T
     for p, copy in enumerate(copies):
@@ -113,7 +113,7 @@
     edge = jnp.zeros((DATES, 128), jnp.float32)
     for m in range(MAPS):
         edge = jnp.where((lanes - HALO_LANE) // 2 == m, out[DATES * m : DATES * m + DATES, :], edge)
-    edge_ref[...] = jnp.where(lanes >= HALO_LANE, edge, 0.0)
+    edge_ref[...] = edge
 
 
 def edge_looks(offsets, tiles):

time: 54.7 us -> 54.7 us (level)
  no operation moved by 1% of the time
where the time goes in v8:
time: 54.7 us; the launch traced here: 54.5 us
  blocking collectives  45 us (82%)
  Pallas kernels  4.75 us (9%)
  waiting for transfers between devices  2.12 us (4%)
  starting transfers between devices  1.92 us (4%)
  between operations  0.66 us (1%)
    all_to_all x1, blocking collectives, shards(): lax.all_to_all(tiles.reshape(DATES, 32, 128), 'date', 0, 0, tiled=True)  29.7 us
    all_to_all x1, blocking collectives, shards(): lax.all_to_all(looks.reshape(DATES, 4, 128), 'date', 0, 0, tiled=True)  15.3 us
    pallas_call x1, Pallas kernels, local_looks(): pl.pallas_call(looks_kernel, out_shape=pltpu.VMEM((4 * DATES, 128), jnp.f...  2.21 us
    ppermute x1, waiting for transfers between devices, shards(): lax.ppermute(edge, ('date', 'col'), edge_pairs(DATES, lax.axis_size('col')))  2.12 us
    ppermute x1, starting transfers between devices, shards(): lax.ppermute(edge, ('date', 'col'), edge_pairs(DATES, lax.axis_size('col')))  1.92 us
  transfers between devices with their start and end apart: 1, of which 1 were waited for; matrix products, arithmetic and copies ran while one was open for 0% of the time, Pallas kernels for 4%

profile of v8, /device:TPU:32, one launch (start us, length us, event | category | flops | bytes accessed | tf_op | source)
XLA Modules:
  0.0 54.5 jit_solution(13990610739473500561)
XLA Ops:
  0.6 1.1 %pieces.1 = (f32[16,2,2,2,8,128]{5,4,3,2,1,0:T(8,128)S(1)}, s32[32,4]{1,0:T(8,128)S(1)}) custom-call(f32[2,16,2,2,8,128]{5,4,3,2,1,0:T(8,128)} %bitcast.13, s32[4,32]{1,0:T(4,128)} %bitcast.14), custom_call_target="tpu_custom_call" | custom-call | tf_op jit(solution)/shard_map/pieces/pallas_call | solution.py:56
  1.7 29.7 %all_to_all.10 = f32[32,32,128]{2,1,0:T(8,128)S(1)} all-to-all(f32[32,32,128]{2,1,0:T(8,128)S(1)} %bitcast.11), channel_id=1, replica_groups=mesh['date'=32,'col'=16] {'date'}, dimensions={0} | all-to-all | bytes 1048576 | tf_op jit(solution)/shard_map/all_to_all | solution.py:317
  31.4 0.4 edge_looks.1
  31.8 1.9 %collective-permute-start = (f32[32,128]{1,0:T(8,128)S(1)}, f32[32,128]{1,0:T(8,128)S(1)}, u32[]{:S(2)}, u32[]{:S(2)}) collective-permute-start(f32[32,128]{1,0:T(8,128)S(1)} %edge_looks.1), channel_id=1, source_target_pairs={{17,16},{16,17},{49,48},{48,49},{81,80},{80,81},{113,112},{112,113... | collective-permute-start | bytes 49160 | tf_op jit(solution)/shard_map/ppermute | solution.py:320
  33.7 2.2 %looks.1.looks_ref = f32[128,128]{1,0:T(8,128)S(1)} custom-call(s32[32,4]{1,0:T(8,128)S(1)} %get-tuple-element.4.offs_smem.offs_ref, s32[32,4]{1,0:T(8,128)S(1)} %get-tuple-element.4.offs_smem.offs_ref, f32[1024,128]{1,0:T(8,128)S(1)} %bitcast.9), custom_call_target="tpu_custom_call" | custom-call | tf_op jit(solution)/shard_map/looks/pallas_call | solution.py:206
  35.9 2.1 %collective-permute-done.edge_ref = f32[32,128]{1,0:T(8,128)S(1)} collective-permute-done((f32[32,128]{1,0:T(8,128)S(1)}, f32[32,128]{1,0:T(8,128)S(1)}, u32[]{:S(2)}, u32[]{:S(2)}) %collective-permute-start) | collective-permute-done | bytes 16416 | tf_op jit(solution)/shard_map/ppermute | solution.py:320
  38.0 15.3 %all_to_all.11 = f32[32,4,128]{2,1,0:T(4,128)S(1)} all-to-all(f32[32,4,128]{2,1,0:T(4,128)S(1)} %bitcast.10), channel_id=1, replica_groups=mesh['date'=32,'col'=16] {'date'}, dimensions={0} | all-to-all | bytes 131072 | tf_op jit(solution)/shard_map/all_to_all | solution.py:322
  53.4 1.1 %finish.1 = (f32[2,1,4,32,32]{4,3,2,1,0:T(8,128)}, f32[1,4,32,32]{3,2,1,0:T(8,128)}) custom-call(s32[32,4]{1,0:T(8,128)S(1)} %get-tuple-element.4.offs_smem.offs_ref, f32[128,128]{1,0:T(8,128)S(1)} %bitcast.12), custom_call_target="tpu_custom_call" | custom-call | tf_op jit(solution)/shard_map/finish/pallas_call | solution.py:289
  (1 shorter events, 0.0 us)
Async XLA Ops:
  31.8 6.3 %collective-permute-start = (f32[32,128]{1,0:T(8,128)S(1)}, f32[32,128]{1,0:T(8,128)S(1)}, u32[]{:S(2)}, u32[]{:S(2)}) collective-permute-start(f32[32,128]{1,0:T(8,128)S(1)} %edge_looks.1), channel_id=1, source_target_pairs={{17,16},{16,17},{49,48},{48,49},{81,80},{80,81},{113,112},{112,113... | collective-permute-start | bytes 49160 | tf_op jit(solution)/shard_map/ppermute | solution.py:320
